TPU v7x, 32 devices: a whole 2x2x4 slice. The times are simulated.
32 devices in a mesh: dp: 8 (over z, y), tensor: 4 (over x, core).
Axes of the slice: x: 2, y: 2, z: 4, core: 2. Of those that a mesh axis runs over, the one named last changes fastest.
Arguments:
- signal: bfloat16 [26112, 512], P('dp', 'tensor'), may hold values from -6 to 6
- horizon: int32 [32], P('dp'), may hold values from 96 to 720, as said below
- down_a: bfloat16 [6144, 512], P('dp', 'tensor'), may hold values from -0.078125 to 0.078125
- iso_a: bfloat16 [34816, 512], P('dp', 'tensor'), may hold values from -0.046875 to 0.046875
- up_a: bfloat16 [512, 12, 512], P('dp', None, 'tensor'), may hold values from -0.25 to 0.25
- down_b: bfloat16 [8192, 512], P('dp', 'tensor'), may hold values from -0.0625 to 0.0625
- iso_b: bfloat16 [26112, 512], P('dp', 'tensor'), may hold values from -0.0546875 to 0.0546875
- up_b: bfloat16 [512, 16, 512], P('dp', None, 'tensor'), may hold values from -0.25 to 0.25
- merge_w: bfloat16 [1024, 512], P('dp', 'tensor'), may hold values from -0.1875 to 0.1875
- ff_in: bfloat16 [512, 2048], P(None, 'tensor'), may hold values from -0.25 to 0.25
- ff_out: bfloat16 [2048, 512], P('tensor'), may hold values from -0.125 to 0.125
- norm_gain: float32 [512], P('tensor'), may hold values from 0.1 to 1.9
- norm_bias: float32 [512], P('tensor'), may hold values from -4 to 4
- first_gain: float32 [512], P('tensor'), may hold values from 0.1 to 1.9
- first_bias: float32 [512], P('tensor'), may hold values from -4 to 4
- last_gain: float32 [512], P('tensor'), may hold values from 0.1 to 1.9
- last_bias: float32 [512], P('tensor'), may hold values from -4 to 4
- cotangent: bfloat16 [26112, 512], P('dp', 'tensor'), may hold values from -6 to 6
Outputs:
- series_out: bfloat16 [26112, 512], P('dp', 'tensor')
- grad_input: float32 [26112, 512], P('dp', 'tensor')
- grad_down_a: float32 [6144, 512], P('dp', 'tensor')
- grad_iso_a: float32 [34816, 512], P('dp', 'tensor')
- grad_up_a: float32 [512, 12, 512], P('dp', None, 'tensor')
- grad_down_b: float32 [8192, 512], P('dp', 'tensor')
- grad_iso_b: float32 [26112, 512], P('dp', 'tensor')
- grad_up_b: float32 [512, 16, 512], P('dp', None, 'tensor')
- grad_merge: float32 [1024, 512], P('dp', 'tensor')
- grad_ff_in: float32 [512, 2048], P(None, 'tensor')
- grad_ff_out: float32 [2048, 512], P('tensor')
- grad_norm_gain: float32 [512], P('tensor')
- grad_norm_bias: float32 [512], P('tensor')
- grad_first_gain: float32 [512], P('tensor')
- grad_first_bias: float32 [512], P('tensor')
- grad_last_gain: float32 [512], P('tensor')
- grad_last_bias: float32 [512], P('tensor')
Inputs may be any that keep to these rules, and one draw needn't show every extreme that they name: Each series' horizon is one of 96, 192, 336 and 720; some series has 720.
All inputs are finite; a program needn't handle non-finite values.
Results may differ from a plain program's by a relative error of at most 0.014.
Values may be sent and summed in bfloat16 or wider, within the bound.
No kernel may reach another device: no remote copies, remote signals or barrier semaphores. Data moves between devices by JAX's collectives and lax.ppermute only.
A program may use at most 384 MiB of HBM per device.

v0:
```python
from functools import partial
import jax
import jax.numpy as jnp
from jax import lax
from jax.sharding import PartitionSpec as P

D = 512
SA = 12
SB = 16
IN_LEN = 96
L = 816
MA = 68
MB = 51
EPS = 1e-05
BF = jnp.bfloat16
F32 = jnp.float32


def matmul(left, right):
    return jnp.dot(left, right, preferred_element_type=F32)


def over_rows(left, right):
    return lax.dot_general(left, right, (((0,), (0,)), ((), ())), preferred_element_type=F32)


def against(left, right):
    return lax.dot_general(left, right, (((1,), (1,)), ((), ())), preferred_element_type=F32)


def swap(value, mask):
    return lax.ppermute(value, "tensor", [(i, i ^ mask) for i in range(4)])


def by_xor(blocks):
    t = lax.axis_index("tensor")
    low = t % 2 == 0
    high = t // 2 == 0
    mid = [jnp.where(low, blocks[k], blocks[k ^ 1]) for k in range(4)]
    return [jnp.where(high, mid[k], mid[k ^ 2]) for k in range(4)]


def lanes(value):
    width = value.shape[1] // 4
    return [value[:, i * width : (i + 1) * width] for i in range(4)]


def own_lanes(value):
    width = value.shape[1] // 4
    return lax.dynamic_slice_in_dim(value, lax.axis_index("tensor") * width, width, 1)


def gather_blocks(value):
    across = swap(value, 2)
    return by_xor([value, swap(value, 1), across, swap(across, 1)])


def channel_gather(value):
    return jnp.concatenate(gather_blocks(value), axis=1)


def to_rows(value):
    t = lax.axis_index("tensor")
    count = value.shape[0] // 4
    send = [lax.dynamic_slice_in_dim(value, (t ^ k) * count, count, 0) for k in range(4)]
    return jnp.concatenate(by_xor([send[0]] + [swap(send[k], k) for k in (1, 2, 3)]), axis=1)


def to_channels(value):
    send = by_xor(lanes(value))
    return jnp.concatenate(by_xor([send[0]] + [swap(send[k], k) for k in (1, 2, 3)]), axis=0)


def quarter_sum(blocks):
    send = by_xor(blocks)
    mine = send[0] + swap(send[1].astype(BF), 1).astype(F32)
    other = send[2] + swap(send[3].astype(BF), 1).astype(F32)
    return mine + swap(other.astype(BF), 2).astype(F32)


def ring_order(count):
    return list(range(0, count, 2)) + list(range(1, count, 2))[::-1]


def ring_gather(value):
    count = lax.axis_size("dp")
    order = ring_order(count)
    table = jnp.array(order, jnp.int32)
    place = jnp.array([order.index(i) for i in range(count)], jnp.int32)[lax.axis_index("dp")]
    up = [(order[i], order[(i + 1) % count]) for i in range(count)]
    down = [(b, a) for a, b in up]
    result = jnp.zeros((count,) + value.shape, value.dtype)
    result = lax.dynamic_update_index_in_dim(result, value, lax.axis_index("dp"), 0)
    ahead = behind = value
    for step in range(1, count // 2 + 1):
        ahead = lax.ppermute(ahead, "dp", up)
        result = lax.dynamic_update_index_in_dim(result, ahead, table[(place - step) % count], 0)
        if step <= (count - 1) // 2:
            behind = lax.ppermute(behind, "dp", down)
            result = lax.dynamic_update_index_in_dim(
                result, behind, table[(place + step) % count], 0
            )
    return result


def exchange_sum(blocks):
    got = lax.all_to_all(blocks.astype(BF), "dp", 0, 0, tiled=True)
    return jnp.sum(got.astype(F32), axis=0)


def scatter_sum(value):
    return lax.psum_scatter(value.astype(BF), "dp", scatter_dimension=0, tiled=True).astype(F32)


def norm_forward(operand, gain_vec, bias_vec):
    row_mean = jnp.mean(operand, axis=1, keepdims=True)
    row_square = jnp.mean(operand * operand, axis=1, keepdims=True)
    inv_std = lax.rsqrt(row_square - row_mean * row_mean + EPS)
    normed = (operand - row_mean) * inv_std
    return (normed * gain_vec + bias_vec, (normed, inv_std))


def norm_backward(upstream, gain_vec, stored):
    normed, inv_std = stored
    scaled = upstream * gain_vec
    first_mean = jnp.mean(scaled, axis=1, keepdims=True)
    second_mean = jnp.mean(scaled * normed, axis=1, keepdims=True)
    result = inv_std * (scaled - first_mean - normed * second_mean)
    return (result, jnp.sum(upstream * normed, axis=0), jnp.sum(upstream, axis=0))


def tap_plan(rows_held):
    count = lax.axis_size("dp")
    taps = max((-(-(i * rows_held % D + rows_held) // D) for i in range(count)))
    start = lax.axis_index("dp") * rows_held
    return (taps, start // D, start % D)


def iso_forward(act_all, weight, span_len):
    groups = act_all.shape[0]
    series = act_all.shape[1] // span_len
    taps, first, offset = tap_plan(weight.shape[0])
    wide = lax.dynamic_update_slice_in_dim(
        jnp.zeros((taps * D, weight.shape[1]), BF), weight, offset, 0
    )
    timed = act_all.reshape(groups, series, span_len, D).transpose(2, 0, 1, 3)
    timed = timed.reshape(span_len, groups * series, D)
    timed = jnp.pad(timed, ((span_len - 1, taps), (0, 0), (0, 0)))
    timed = lax.dynamic_slice_in_dim(timed, first, span_len + taps - 1, 0)
    columns = jnp.concatenate([timed[j : j + span_len] for j in range(taps)], axis=2)
    columns = columns.reshape(span_len * groups * series, taps * D)
    pre = matmul(columns, wide).reshape(span_len, groups, series, -1)
    pre = pre.transpose(1, 2, 0, 3).reshape(groups, series * span_len, -1)
    return (pre, (columns, wide))


def iso_backward(grad_all, stored, rows_held, span_len):
    columns, wide = stored
    groups = grad_all.shape[0]
    series = grad_all.shape[1] // span_len
    taps, first, offset = tap_plan(rows_held)
    timed = grad_all.reshape(groups, series, span_len, -1).transpose(2, 0, 1, 3)
    timed = timed.reshape(span_len * groups * series, -1)
    grad_wide = over_rows(columns, timed)
    grad_weight = lax.dynamic_slice_in_dim(grad_wide, offset, rows_held, 0)
    spread = against(timed, wide).reshape(span_len, groups * series, taps * D)
    total = jnp.zeros((span_len + taps - 1, groups * series, D), F32)
    for j in range(taps):
        total = total.at[j : j + span_len].add(spread[:, :, j * D : (j + 1) * D])
    padded = jnp.zeros((2 * span_len - 1 + taps, groups * series, D), F32)
    padded = lax.dynamic_update_slice_in_dim(padded, total, first, 0)
    back = padded[span_len - 1 : 2 * span_len - 1].reshape(span_len, groups, series, D)
    return (grad_weight, back.transpose(1, 2, 0, 3).reshape(groups, series * span_len, D))


def body(
    signal,
    horizon,
    down_a,
    iso_a,
    up_a,
    down_b,
    iso_b,
    up_b,
    merge_w,
    ff_in,
    ff_out,
    norm_gain,
    norm_bias,
    first_gain,
    first_bias,
    last_gain,
    last_bias,
    cotangent,
):
    row_count, col_count = signal.shape
    part_rows = row_count // 4
    series_count = row_count // L
    short_a = row_count // SA
    short_b = row_count // SB
    t = lax.axis_index("tensor")
    wd_a = ring_gather(down_a).reshape(SA * D, col_count)
    wd_b = ring_gather(down_b).reshape(SB * D, col_count)
    x_full = channel_gather(signal)
    vectors = channel_gather(
        jnp.stack([norm_gain, norm_bias, first_gain, first_bias, last_gain, last_bias])
    )
    n_gain, n_bias, f_gain, f_bias, l_gain, l_bias = (vectors[i : i + 1] for i in range(6))
    cot_rows = to_rows(cotangent)
    wu_a = lax.all_gather(up_a, "dp", axis=0, tiled=True).reshape(D, SA * col_count)
    wu_b = lax.all_gather(up_b, "dp", axis=0, tiled=True).reshape(D, SB * col_count)
    w_merge = channel_gather(ring_gather(merge_w).reshape(2 * D, col_count))
    w_in = channel_gather(ff_in)
    w_out = jnp.concatenate(gather_blocks(ff_out), axis=0)
    window_a = x_full.reshape(short_a, SA * D)
    window_b = x_full.reshape(short_b, SB * D)
    down_act = jnp.concatenate(
        [jnp.tanh(matmul(window_a, wd_a)), jnp.tanh(matmul(window_b, wd_b))], axis=0
    )
    down_low = down_act.astype(BF)
    high = t // 2 == 0
    low = t % 2 == 0
    across = swap(down_low, 2)
    pair = jnp.concatenate(
        [jnp.where(high, down_low, across), jnp.where(high, across, down_low)], axis=1
    )
    pair_all = ring_gather(pair)
    mate_all = swap(pair_all, 1)
    even = jnp.where(low, pair_all, mate_all)
    odd = jnp.where(low, mate_all, pair_all)
    down_all = jnp.concatenate(
        [even[..., :col_count], odd[..., :col_count], even[..., col_count:], odd[..., col_count:]],
        axis=2,
    )
    down_full = lax.dynamic_index_in_dim(down_all, lax.axis_index("dp"), 0, keepdims=False)
    part_a, iso_store_a = iso_forward(down_all[:, :short_a], iso_a, MA)
    part_b, iso_store_b = iso_forward(down_all[:, short_a:], iso_b, MB)
    iso_pre = exchange_sum(jnp.concatenate([part_a, part_b], axis=1))
    iso_act = jnp.tanh(channel_gather(iso_pre))
    middle, store_mid = norm_forward(iso_act + down_full.astype(F32), n_gain, n_bias)
    middle = middle.astype(BF)
    up_act_a = jnp.tanh(matmul(middle[:short_a], wu_a).reshape(row_count, col_count))
    up_act_b = jnp.tanh(matmul(middle[short_a:], wu_b).reshape(row_count, col_count))
    x_rows = lax.dynamic_slice_in_dim(x_full, t * part_rows, part_rows, 0).astype(F32)
    branch_a, store_br_a = norm_forward(
        to_rows(up_act_a.astype(BF)).astype(F32) + x_rows, n_gain, n_bias
    )
    branch_b, store_br_b = norm_forward(
        to_rows(up_act_b.astype(BF)).astype(F32) + x_rows, n_gain, n_bias
    )
    merge_in = jnp.concatenate([branch_a.astype(BF), branch_b.astype(BF)], axis=1)
    merged = matmul(merge_in, w_merge)
    first_out, store_first = norm_forward(merged, f_gain, f_bias)
    first_low = first_out.astype(BF)
    hidden_pre = matmul(first_low, w_in)
    hidden = jax.nn.gelu(hidden_pre, approximate=False).astype(BF)
    feed = matmul(hidden, w_out)
    last_out, store_last = norm_forward(merged + feed, l_gain, l_bias)
    position = t * part_rows + lax.broadcasted_iota(jnp.int32, (part_rows, 1), 0)
    limit = jnp.broadcast_to(horizon[:, None], (series_count, L)).reshape(row_count, 1)
    limit = lax.dynamic_slice_in_dim(limit, t * part_rows, part_rows, 0)
    out_mask = (position % L < IN_LEN + limit).astype(F32)
    series_out = to_channels((last_out * out_mask).astype(BF))
    upstream = cot_rows.astype(F32) * out_mask
    grad_sum, grad_last_gain, grad_last_bias = norm_backward(upstream, l_gain, store_last)
    grad_feed = grad_sum.astype(BF)
    grad_ff_out = over_rows(hidden, grad_feed)
    grad_hidden = against(grad_feed, w_out)
    _, gelu_back = jax.vjp(partial(jax.nn.gelu, approximate=False), hidden_pre)
    grad_hpre = gelu_back(grad_hidden)[0].astype(BF)
    grad_ff_in = over_rows(first_low, grad_hpre)
    grad_first = against(grad_hpre, w_in)
    grad_merged_norm, grad_first_gain, grad_first_bias = norm_backward(
        grad_first, f_gain, store_first
    )
    grad_merged = (grad_merged_norm + grad_sum).astype(BF)
    grad_merge = over_rows(merge_in, grad_merged)
    grad_pair = against(grad_merged, w_merge)
    grad_resid_a, gain_one, bias_one = norm_backward(grad_pair[:, :D], n_gain, store_br_a)
    grad_resid_b, gain_two, bias_two = norm_backward(grad_pair[:, D:], n_gain, store_br_b)
    resid_a = to_channels(grad_resid_a.astype(BF)).astype(F32)
    resid_b = to_channels(grad_resid_b.astype(BF)).astype(F32)
    grad_upre_a = (resid_a * (1.0 - up_act_a * up_act_a)).astype(BF).reshape(short_a, -1)
    grad_upre_b = (resid_b * (1.0 - up_act_b * up_act_b)).astype(BF).reshape(short_b, -1)
    part_mid = jnp.concatenate([against(grad_upre_a, wu_a), against(grad_upre_b, wu_b)], axis=0)
    grad_up_a = over_rows(middle[:short_a], grad_upre_a).reshape(D, SA, col_count)
    grad_up_b = over_rows(middle[short_a:], grad_upre_b).reshape(D, SB, col_count)
    blocks = lanes(part_mid)
    keep = jnp.concatenate(
        [jnp.where(low, blocks[0], blocks[1]), jnp.where(low, blocks[2], blocks[3])], axis=1
    )
    give = jnp.concatenate(
        [jnp.where(low, blocks[1], blocks[0]), jnp.where(low, blocks[3], blocks[2])], axis=1
    )
    keep = keep + swap(give, 1)
    keep = keep + swap(keep, 2)
    mate = swap(keep, 1)
    even = jnp.where(low, keep, mate)
    odd = jnp.where(low, mate, keep)
    grad_middle = jnp.concatenate(
        [even[:, :col_count], odd[:, :col_count], even[:, col_count:], odd[:, col_count:]], axis=1
    )
    grad_inner, gain_mid, bias_mid = norm_backward(grad_middle, n_gain, store_mid)
    grad_ipre = own_lanes((grad_inner * (1.0 - iso_act * iso_act)).astype(BF))
    grad_ipre_all = ring_gather(grad_ipre)
    grad_iso_a, back_a = iso_backward(grad_ipre_all[:, :short_a], iso_store_a, iso_a.shape[0], MA)
    grad_iso_b, back_b = iso_backward(grad_ipre_all[:, short_a:], iso_store_b, iso_b.shape[0], MB)
    back = jnp.concatenate([back_a, back_b], axis=1)
    groups = back.shape[0]
    back = quarter_sum([back[..., i * col_count : (i + 1) * col_count] for i in range(4)])
    grad_down = exchange_sum(back)
    grad_dpre = ((grad_down + own_lanes(grad_inner)) * (1.0 - down_act * down_act)).astype(BF)
    grad_dpre_a, grad_dpre_b = (grad_dpre[:short_a], grad_dpre[short_a:])
    grad_down_a = over_rows(window_a, grad_dpre_a)
    grad_down_b = over_rows(window_b, grad_dpre_b)
    grad_x = against(grad_dpre_a, wd_a).reshape(row_count, D) + against(grad_dpre_b, wd_b).reshape(
        row_count, D
    )
    grad_input = quarter_sum(lanes(grad_x)) + resid_a + resid_b
    sum_up_a = scatter_sum(grad_up_a)
    sum_up_b = scatter_sum(grad_up_b)
    sum_down_a = scatter_sum(grad_down_a)
    sum_down_b = scatter_sum(grad_down_b)
    sum_merge = scatter_sum(quarter_sum(lanes(grad_merge)))
    ff_own = jnp.concatenate(
        [
            quarter_sum(lanes(grad_ff_in)),
            quarter_sum([grad_ff_out[i * D : (i + 1) * D] for i in range(4)]),
        ],
        axis=0,
    )
    ff_total = ring_gather(scatter_sum(ff_own).astype(BF)).reshape(2 * D, D).astype(F32)
    sums = jnp.stack(
        [
            gain_one + gain_two + 0.25 * gain_mid,
            bias_one + bias_two + 0.25 * bias_mid,
            grad_first_gain,
            grad_first_bias,
            grad_last_gain,
            grad_last_bias,
        ]
    )
    sums = own_lanes(lax.psum(sums, ("dp", "tensor")))
    return (
        series_out,
        grad_input,
        sum_down_a,
        grad_iso_a,
        sum_up_a,
        sum_down_b,
        grad_iso_b,
        sum_up_b,
        sum_merge,
        ff_total[:D],
        ff_total[D:],
        sums[0],
        sums[1],
        sums[2],
        sums[3],
        sums[4],
        sums[5],
    )


def solution(mesh):
    in_specs = (
        P("dp", "tensor"),
        P("dp"),
        P("dp", "tensor"),
        P("dp", "tensor"),
        P("dp", None, "tensor"),
        P("dp", "tensor"),
        P("dp", "tensor"),
        P("dp", None, "tensor"),
        P("dp", "tensor"),
        P(None, "tensor"),
        P("tensor", None),
        P("tensor"),
        P("tensor"),
        P("tensor"),
        P("tensor"),
        P("tensor"),
        P("tensor"),
        P("dp", "tensor"),
    )
    out_specs = (
        P("dp", "tensor"),
        P("dp", "tensor"),
        P("dp", "tensor"),
        P("dp", "tensor"),
        P("dp", None, "tensor"),
        P("dp", "tensor"),
        P("dp", "tensor"),
        P("dp", None, "tensor"),
        P("dp", "tensor"),
        P(None, "tensor"),
        P("tensor", None),
        P("tensor"),
        P("tensor"),
        P("tensor"),
        P("tensor"),
        P("tensor"),
        P("tensor"),
    )
    return jax.shard_map(body, mesh=mesh, in_specs=in_specs, out_specs=out_specs, check_vma=False)
```

profile of v0, /device:TPU:0, one launch (start us, length us, event | category | flops | bytes accessed | tf_op | source)
XLA Modules:
  0.0 962.9 jit_solution(12522362180640404888)
XLA Ops:
  41.1 11.8 %collective-permute-done.11 = bf16[1024,128]{1,0:T(8,128)(2,1)S(1)} collective-permute-done((bf16[1024,128]{1,0:T(8,128)(2,1)S(1)}, bf16[1024,128]{1,0:T(8,128)(2,1)S(1)}, u32[]{:S(2)}, u32[]{:S(2)}) %collective-permute-start.11) | collective-permute-done | bytes 262176 | tf_op jit(solution)/shard_map/ppermute | solution.py:99
  55.0 6.5 collective-permute-done.6
  80.7 4.2 collective-permute-done.16
  87.6 5.0 reshape.927
  95.9 3.6 convolution_tanh_fusion.2
  101.8 4.3 collective-permute-done.17
  109.8 3.5 collective-permute-done.18
  113.4 3.6 collective-permute-done.19
  120.4 10.6 %collective-permute-done.21 = bf16[476,256]{1,0:T(8,128)(2,1)S(1)} collective-permute-done((bf16[476,256]{1,0:T(8,128)(2,1)S(1)}, bf16[476,256]{1,0:T(8,128)(2,1)S(1)}, u32[]{:S(2)}, u32[]{:S(2)}) %collective-permute-start.21) | collective-permute-done | bytes 243744 | tf_op jit(solution)/shard_map/ppermute | solution.py:99
  133.2 5.9 collective-permute-done.23
  172.6 21.0 %fusion.53 = bf16[8,4,68,128]{3,2,1,0:T(8,128)(2,1)S(1)} fusion(bf16[68,8,4,4608]{3,0,2,1:T(8,128)(2,1)S(1)} %bitcast.258, bf16[4608,128]{1,0:T(8,128)(2,1)} %constant_dynamic-update-slice_fusion), kind=kOutput, calls=%fused_computation.173 | convolution fusion | flops 2567192576 | bytes 21790720 | tf_op jit(solution)/shard_map/dot_general | solution.py:20
  212.4 22.6 %dot_general.101 = bf16[51,8,4,4096]{3,2,1,0:T(4,128)(2,1)} reshape(bf16[51,32,4096]{2,1,0:T(8,128)(2,1)} %fusion.38) | data formatting | bytes 26738688 | tf_op jit(solution)/shard_map/dot_general | solution.py:20
  235.0 10.3 %fusion.54 = bf16[8,4,51,128]{3,1,0,2:T(4,128)(2,1)S(1)} fusion(bf16[51,8,4,4096]{3,2,1,0:T(4,128)(2,1)} %dot_general.101, bf16[4096,128]{1,0:T(8,128)(2,1)} %constant_dynamic-update-slice_fusion.2), kind=kOutput, calls=%fused_computation.174 | convolution fusion | flops 1711484928 | bytes 14835712 | tf_op jit(solution)/shard_map/dot_general | solution.py:20
  246.6 4.5 all-to-all-start
  253.2 13.6 %collective-permute-done.42 = bf16[128,128]{1,0:T(8,128)(2,1)S(1)} collective-permute-done((bf16[128,128]{1,0:T(8,128)(2,1)S(1)}, bf16[128,128]{1,0:T(8,128)(2,1)S(1)}, u32[]{:S(2)}, u32[]{:S(2)}) %collective-permute-start.42) | collective-permute-done | bytes 32800 | tf_op jit(solution)/shard_map/ppermute | solution.py:96
  266.9 8.5 collective-permute-done.43
  284.2 4.9 collective-permute-done.58
  289.1 5.6 collective-permute-done.46
  294.7 3.7 collective-permute-done.59
  307.3 3.7 collective-permute-done.27
  319.3 3.5 fusion.116
  339.8 4.0 collective-permute-done.33
  350.4 19.4 %multiply_convert_fusion = (bf16[816,2048]{1,0:T(8,128)(2,1)S(1)}, f32[816,2048]{1,0:T(8,128)}, f32[816,2048]{1,0:T(8,128)}) fusion(bf16[512,512]{1,0:T(8,128)(2,1)S(1)} %copy-done.71, bf16[512,512]{1,0:T(8,128)(2,1)S(1)} %copy-done.70, bf16[512,512]{1,0:T(8,128)(2,1)S(1)} %copy-done.69, bf16[512,512]{1,0:T(8,128)(2,1)S(1)} %copy-done.68, ...), kind=kOutput, calls=%fused_computation.28 | convolution fusion | flops 1830379520 | bytes 20490624 | tf_op jit(solution)/shard_map/dot_general | solution.py:20
  373.6 7.2 add_convert_fusion
  445.6 18.4 %collective-permute-done.67 = f32[476,256]{1,0:T(8,128)} collective-permute-done((f32[476,256]{1,0:T(8,128)}, f32[476,256]{1,0:T(8,128)}, u32[]{:S(2)}, u32[]{:S(2)}) %collective-permute-start.67) | collective-permute-done | bytes 487456 | tf_op jit(solution)/shard_map/ppermute | solution.py:32
  468.7 5.5 collective-permute-done.90
  491.9 21.0 %copy.121 = bf16[68,32,4608]{2,1,0:T(8,128)(2,1)} copy(bf16[68,32,4608]{2,0,1:T(8,128)(2,1)} %copy-done.11) | data formatting | bytes 40108032 | tf_op jit(solution)/shard_map/concatenate | solution.py:150
  518.0 6.4 dynamic_update_slice.196
  524.8 6.4 dynamic_update_slice.197
  531.2 6.4 dynamic_update_slice.198
  538.0 6.4 dynamic_update_slice.199
  544.4 6.4 dynamic_update_slice.200
  551.3 6.4 dynamic_update_slice.201
  557.7 6.4 dynamic_update_slice.202
  564.3 6.4 dynamic_update_slice.203
  571.1 17.3 %fusion.56 = f32[68,32,4608]{2,1,0:T(8,128)} fusion(bf16[68,32,128]{2,1,0:T(8,128)(2,1)S(1)} %bitcast.272, bf16[4608,128]{1,0:T(8,128)(2,1)} %constant_dynamic-update-slice_fusion), kind=kOutput, calls=%fused_computation.176 | convolution fusion | flops 2566914048 | bytes 41844736 | tf_op jit(solution)/shard_map/dot_general | solution.py:28
  591.6 3.5 fusion.13
  595.1 3.5 fusion.12
  602.1 3.5 fusion.10
  605.5 3.5 fusion.9
  612.4 3.5 fusion.7
  619.4 5.5 copy.116
  624.9 4.9 broadcast_in_dim.247
  629.8 22.3 %dynamic_update_slice.204 = f32[144,32,512]{2,0,1:T(8,128)} dynamic-update-slice(f32[144,32,512]{2,0,1:T(8,128)} %broadcast_in_dim.247, f32[76,32,512]{2,0,1:T(8,128)} %copy.116, s32[]{:T(128)S(6)} %select_n.1414, s32[]{:T(128)} %constant.1016.clone.1, s32[]{:T(128)} %constant.1016.clone.1) | dynamic-update-slice | bytes 9961476 | tf_op jit(solution)/shard_map/dynamic_update_slice | solution.py:171
  655.2 4.6 copy.117
  659.9 12.2 %fusion.61 = f32[51,32,4096]{2,1,0:T(8,128)} fusion(bf16[51,32,128]{2,1,0:T(8,128)(2,1)S(1)} %bitcast.274, bf16[4096,128]{1,0:T(8,128)(2,1)} %constant_dynamic-update-slice_fusion.2), kind=kOutput, calls=%fused_computation.185 | convolution fusion | flops 1711276032 | bytes 28205056 | tf_op jit(solution)/shard_map/dot_general | solution.py:28
  677.8 3.5 fusion.19
  697.5 3.9 select_convert_fusion.1
  725.6 53.8 %psum.7 = f32[6,512]{1,0:T(8,128)S(1)} all-reduce(f32[6,512]{1,0:T(8,128)S(1)} %stack.49), channel_id=1, replica_groups=mesh['dp'=8,'tensor'=4] {'dp','tensor'}, use_global_device_ids=true, to_apply=%region_38.39 | all-reduce | flops 3072 | bytes 24576 | tf_op jit(solution)/shard_map/psum | solution.py:343
  783.5 4.9 all-to-all-start.1
  788.4 7.0 fusion.119
  796.8 16.2 %all-to-all-done.1 = bf16[8,476,128]{2,1,0:T(8,128)(2,1)} async-done(((bf16[8,476,128]{2,1,0:T(8,128)(2,1)}), bf16[8,476,128]{2,1,0:T(8,128)(2,1)}, u32[]{:S(2)}, u32[]{:S(2)}) %all-to-all-start.1) | async-done | bytes 974880 | tf_op jit(solution)/shard_map/all_to_all | solution.py:107
  818.8 10.2 %fusion.118 = f32[4608,128]{1,0:T(8,128)S(1)} fusion(bf16[2176,4608]{1,0:T(8,128)(2,1)} %bitcast.259, bf16[2176,128]{1,0:T(8,128)(2,1)} %bitcast.273), kind=kOutput, calls=%fused_computation.513 | convolution fusion | flops 2566914048 | bytes 22970368 | tf_op jit(solution)/shard_map/dot_general | solution.py:24
  840.2 3.9 fusion.89
  844.1 8.4 reshape.948
  852.4 3.8 fusion.86
  856.2 7.9 reshape.947
  864.2 9.4 add.1215
  876.3 4.3 select_convert_fusion.3
  886.3 4.1 collective-permute-done.95
  890.4 4.3 add_convert_fusion.3
  899.9 16.2 %collective-permute-done.81 = bf16[3264,128]{1,0:T(8,128)(2,1)} collective-permute-done((bf16[3264,128]{1,0:T(8,128)(2,1)}, bf16[3264,128]{1,0:T(8,128)(2,1)}, u32[]{:S(2)}, u32[]{:S(2)}) %collective-permute-start.81) | collective-permute-done | bytes 835616 | tf_op jit(solution)/shard_map/ppermute | solution.py:32
  916.2 8.2 add_add_fusion
  926.1 27.7 %reduce-scatter.11.cloned.1.call-done = bf16[1024,128]{1,0:T(8,128)(2,1)} async-done(((bf16[8192,128]{1,0:T(8,128)(2,1)}), bf16[1024,128]{1,0:T(8,128)(2,1)}) %reduce-scatter.11.cloned.1.call-update) | async-done | bytes 262160 | tf_op jit(solution)/shard_map/reduce_scatter | solution.py:112
  (646 shorter events, 357.8 us)
Async XLA Ops:
  7.2 306.6 %all-gather.3.cloned.1.call-start = ((), (), s32[]{:S(2)}) async-start(), calls=%async_computation.8 | async-start | bytes 1769472 | tf_op jit(solution)/shard_map/all_gather | solution.py:210
  7.2 29.3 %collective-permute-start.3 = (bf16[768,128]{1,0:T(8,128)(2,1)}, bf16[768,128]{1,0:T(8,128)(2,1)}, u32[]{:S(2)}, u32[]{:S(2)}) collective-permute-start(bf16[768,128]{1,0:T(8,128)(2,1)} %param.66), channel_id=1, source_target_pairs={{0,8},{8,16},{16,24},{24,28},{28,20},{20,12},{12,4},{4,0},{1,9},{9... | collective-permute-start | bytes 589832 | tf_op jit(solution)/shard_map/ppermute | solution.py:96
  10.3 27.7 %collective-permute-start.4 = (bf16[768,128]{1,0:T(8,128)(2,1)}, bf16[768,128]{1,0:T(8,128)(2,1)}, u32[]{:S(2)}, u32[]{:S(2)}) collective-permute-start(bf16[768,128]{1,0:T(8,128)(2,1)} %param.66), channel_id=1, source_target_pairs={{8,0},{16,8},{24,16},{28,24},{20,28},{12,20},{4,12},{0,4},{9,1},{1... | collective-permute-start | bytes 589832 | tf_op jit(solution)/shard_map/ppermute | solution.py:99
  10.3 66.1 %collective-permute-start.1 = (bf16[3264,128]{1,0:T(8,128)(2,1)}, bf16[3264,128]{1,0:T(8,128)(2,1)S(1)}, u32[]{:S(2)}, u32[]{:S(2)}) collective-permute-start(bf16[3264,128]{1,0:T(8,128)(2,1)} %param.64), channel_id=1, source_target_pairs={{0,2},{1,3},{2,0},{3,1},{4,6},{5,7},{6,4},{7,5},{8,10},{9,11},{10,... | collective-permute-start | bytes 2506760 | tf_op jit(solution)/shard_map/ppermute | solution.py:32
  12.3 72.7 %collective-permute-start = (bf16[3264,128]{1,0:T(8,128)(2,1)}, bf16[3264,128]{1,0:T(8,128)(2,1)}, u32[]{:S(2)}, u32[]{:S(2)}) collective-permute-start(bf16[3264,128]{1,0:T(8,128)(2,1)} %param.64), channel_id=1, source_target_pairs={{0,1},{1,0},{2,3},{3,2},{4,5},{5,4},{6,7},{7,6},{8,9},{9,8},{10,11... | collective-permute-start | bytes 2506760 | tf_op jit(solution)/shard_map/ppermute | solution.py:32
  12.3 28.3 %collective-permute-start.10 = (bf16[1024,128]{1,0:T(8,128)(2,1)}, bf16[1024,128]{1,0:T(8,128)(2,1)S(1)}, u32[]{:S(2)}, u32[]{:S(2)}) collective-permute-start(bf16[1024,128]{1,0:T(8,128)(2,1)} %param.69), channel_id=1, source_target_pairs={{0,8},{8,16},{16,24},{24,28},{28,20},{20,12},{12,4},{4,0},{1,9},{9... | collective-permute-start | bytes 786440 | tf_op jit(solution)/shard_map/ppermute | solution.py:96
  13.9 305.4 %all-gather.5.cloned.1.call-start = ((), (), s32[]{:S(2)}) async-start(), calls=%async_computation.9 | async-start | bytes 2359296 | tf_op jit(solution)/shard_map/all_gather | solution.py:211
  36.5 16.4 %collective-permute-start.11 = (bf16[1024,128]{1,0:T(8,128)(2,1)S(1)}, bf16[1024,128]{1,0:T(8,128)(2,1)S(1)}, u32[]{:S(2)}, u32[]{:S(2)}) collective-permute-start(bf16[1024,128]{1,0:T(8,128)(2,1)S(1)} %copy-done.76), channel_id=1, source_target_pairs={{8,0},{16,8},{24,16},{28,24},{20,28},{12,20},{4,12},{0,4},{9,1},{1... | collective-permute-start | bytes 786440 | tf_op jit(solution)/shard_map/ppermute | solution.py:99
  38.0 15.2 %collective-permute-start.5 = (bf16[768,128]{1,0:T(8,128)(2,1)}, bf16[768,128]{1,0:T(8,128)(2,1)S(1)}, u32[]{:S(2)}, u32[]{:S(2)}) collective-permute-start(bf16[768,128]{1,0:T(8,128)(2,1)} %collective-permute-done.3), channel_id=1, source_target_pairs={{0,8},{8,16},{16,24},{24,28},{28,20},{20,12},{12,4},{4,0},{1,9},{9... | collective-permute-start | bytes 589832 | tf_op jit(solution)/shard_map/ppermute | solution.py:96
  40.6 20.9 %collective-permute-start.6 = (bf16[768,128]{1,0:T(8,128)(2,1)}, bf16[768,128]{1,0:T(8,128)(2,1)S(1)}, u32[]{:S(2)}, u32[]{:S(2)}) collective-permute-start(bf16[768,128]{1,0:T(8,128)(2,1)} %collective-permute-done.4), channel_id=1, source_target_pairs={{8,0},{16,8},{24,16},{28,24},{20,28},{12,20},{4,12},{0,4},{9,1},{1... | collective-permute-start | bytes 589832 | tf_op jit(solution)/shard_map/ppermute | solution.py:99
  52.9 10.3 %collective-permute-start.12 = (bf16[1024,128]{1,0:T(8,128)(2,1)S(1)}, bf16[1024,128]{1,0:T(8,128)(2,1)S(1)}, u32[]{:S(2)}, u32[]{:S(2)}) collective-permute-start(bf16[1024,128]{1,0:T(8,128)(2,1)S(1)} %collective-permute-done.10), channel_id=1, source_target_pairs={{0,8},{8,16},{16,24},{24,28},{28,20},{20,12},{12,4},{4,0},{1,9},{9... | collective-permute-start | bytes 786440 | tf_op jit(solution)/shard_map/ppermute | solution.py:96
  53.2 14.9 %collective-permute-start.13 = (bf16[1024,128]{1,0:T(8,128)(2,1)S(1)}, bf16[1024,128]{1,0:T(8,128)(2,1)S(1)}, u32[]{:S(2)}, u32[]{:S(2)}) collective-permute-start(bf16[1024,128]{1,0:T(8,128)(2,1)S(1)} %collective-permute-done.11), channel_id=1, source_target_pairs={{8,0},{16,8},{24,16},{28,24},{20,28},{12,20},{4,12},{0,4},{9,1},{1... | collective-permute-start | bytes 786440 | tf_op jit(solution)/shard_map/ppermute | solution.py:99
  106.9 171.4 %collective-permute-start.30 = (f32[6,128]{1,0:T(8,128)S(1)}, f32[6,128]{1,0:T(8,128)S(1)}, u32[]{:S(2)}, u32[]{:S(2)}) collective-permute-start(f32[6,128]{1,0:T(8,128)S(1)} %stack.44), channel_id=1, source_target_pairs={{0,2},{1,3},{2,0},{3,1},{4,6},{5,7},{6,4},{7,5},{8,10},{9,11},{10,... | collective-permute-start | bytes 9224 | tf_op jit(solution)/shard_map/ppermute | solution.py:32
  107.5 173.6 %collective-permute-start.29 = (f32[6,128]{1,0:T(8,128)S(1)}, f32[6,128]{1,0:T(8,128)S(1)}, u32[]{:S(2)}, u32[]{:S(2)}) collective-permute-start(f32[6,128]{1,0:T(8,128)S(1)} %stack.44), channel_id=1, source_target_pairs={{0,1},{1,0},{2,3},{3,2},{4,5},{5,4},{6,7},{7,6},{8,9},{9,8},{10,11... | collective-permute-start | bytes 9224 | tf_op jit(solution)/shard_map/ppermute | solution.py:32
  107.5 40.9 %collective-permute-start.38 = (bf16[128,128]{1,0:T(8,128)(2,1)S(1)}, bf16[128,128]{1,0:T(8,128)(2,1)S(1)}, u32[]{:S(2)}, u32[]{:S(2)}) collective-permute-start(bf16[128,128]{1,0:T(8,128)(2,1)S(1)} %copy-done.84), channel_id=1, source_target_pairs={{0,8},{8,16},{16,24},{24,28},{28,20},{20,12},{12,4},{4,0},{1,9},{9... | collective-permute-start | bytes 98312 | tf_op jit(solution)/shard_map/ppermute | solution.py:96
  117.0 14.0 %collective-permute-start.21 = (bf16[476,256]{1,0:T(8,128)(2,1)S(1)}, bf16[476,256]{1,0:T(8,128)(2,1)S(1)}, u32[]{:S(2)}, u32[]{:S(2)}) collective-permute-start(bf16[476,256]{1,0:T(8,128)(2,1)S(1)} %collective-permute-done.19), channel_id=1, source_target_pairs={{8,0},{16,8},{24,16},{28,24},{20,28},{12,20},{4,12},{0,4},{9,1},{1... | collective-permute-start | bytes 731144 | tf_op jit(solution)/shard_map/ppermute | solution.py:99
  120.4 10.7 %collective-permute-start.22 = (bf16[476,256]{1,0:T(8,128)(2,1)S(1)}, bf16[476,256]{1,0:T(8,128)(2,1)S(1)}, u32[]{:S(2)}, u32[]{:S(2)}) collective-permute-start(bf16[476,256]{1,0:T(8,128)(2,1)S(1)} %collective-permute-done.20), channel_id=1, source_target_pairs={{0,8},{8,16},{16,24},{24,28},{28,20},{20,12},{12,4},{4,0},{1,9},{9... | collective-permute-start | bytes 731144 | tf_op jit(solution)/shard_map/ppermute | solution.py:96
  139.0 10.9 %collective-permute-start.39 = (bf16[128,128]{1,0:T(8,128)(2,1)S(1)}, bf16[128,128]{1,0:T(8,128)(2,1)S(1)}, u32[]{:S(2)}, u32[]{:S(2)}) collective-permute-start(bf16[128,128]{1,0:T(8,128)(2,1)S(1)} %copy-done.84), channel_id=1, source_target_pairs={{8,0},{16,8},{24,16},{28,24},{20,28},{12,20},{4,12},{0,4},{9,1},{1... | collective-permute-start | bytes 98312 | tf_op jit(solution)/shard_map/ppermute | solution.py:99
  141.7 12.8 %collective-permute-start.25 = (bf16[8,476,256]{2,0,1:T(8,128)(2,1)}, bf16[8,476,256]{2,0,1:T(8,128)(2,1)}, u32[]{:S(2)}, u32[]{:S(2)}) collective-permute-start(bf16[8,476,256]{2,0,1:T(8,128)(2,1)} %copy.96), channel_id=1, source_target_pairs={{0,1},{1,0},{2,3},{3,2},{4,5},{5,4},{6,7},{7,6},{8,9},{9,8},{10,11... | collective-permute-start | bytes 5849096 | tf_op jit(solution)/shard_map/ppermute | solution.py:32
  148.4 150.2 %collective-permute-start.49 = (bf16[512,512]{1,0:T(8,128)(2,1)}, bf16[512,512]{1,0:T(8,128)(2,1)}, u32[]{:S(2)}, u32[]{:S(2)}) collective-permute-start(bf16[512,512]{1,0:T(8,128)(2,1)} %param.73), channel_id=1, source_target_pairs={{0,2},{1,3},{2,0},{3,1},{4,6},{5,7},{6,4},{7,5},{8,10},{9,11},{10,... | collective-permute-start | bytes 1572872 | tf_op jit(solution)/shard_map/ppermute | solution.py:32
  153.9 147.4 %collective-permute-start.52 = (bf16[512,512]{1,0:T(8,128)(2,1)}, bf16[512,512]{1,0:T(8,128)(2,1)}, u32[]{:S(2)}, u32[]{:S(2)}) collective-permute-start(bf16[512,512]{1,0:T(8,128)(2,1)} %param.74), channel_id=1, source_target_pairs={{0,2},{1,3},{2,0},{3,1},{4,6},{5,7},{6,4},{7,5},{8,10},{9,11},{10,... | collective-permute-start | bytes 1572872 | tf_op jit(solution)/shard_map/ppermute | solution.py:32
  154.5 96.7 %collective-permute-start.41 = (bf16[128,128]{1,0:T(8,128)(2,1)S(1)}, bf16[128,128]{1,0:T(8,128)(2,1)S(1)}, u32[]{:S(2)}, u32[]{:S(2)}) collective-permute-start(bf16[128,128]{1,0:T(8,128)(2,1)S(1)} %collective-permute-done.39), channel_id=1, source_target_pairs={{8,0},{16,8},{24,16},{28,24},{20,28},{12,20},{4,12},{0,4},{9,1},{1... | collective-permute-start | bytes 98312 | tf_op jit(solution)/shard_map/ppermute | solution.py:99
  246.6 56.1 %all-to-all-start = ((bf16[8,476,128]{2,1,0:T(8,128)(2,1)}), bf16[8,476,128]{2,1,0:T(8,128)(2,1)S(1)}, u32[]{:S(2)}, u32[]{:S(2)}) async-start(bf16[8,476,128]{2,1,0:T(8,128)(2,1)} %copy.105), calls=%async_computation | async-start | bytes 1966080 | tf_op jit(solution)/shard_map/all_to_all | solution.py:107
  251.1 473.0 %reduce-scatter.15.cloned.1.call-start = ((), (), s32[]{:S(2)}) async-start(), calls=%async_computation.14 | async-start | bytes 294912 | tf_op jit(solution)/shard_map/reduce_scatter | solution.py:112
  251.2 15.7 %collective-permute-start.42 = (bf16[128,128]{1,0:T(8,128)(2,1)S(1)}, bf16[128,128]{1,0:T(8,128)(2,1)S(1)}, u32[]{:S(2)}, u32[]{:S(2)}) collective-permute-start(bf16[128,128]{1,0:T(8,128)(2,1)S(1)} %collective-permute-done.40), channel_id=1, source_target_pairs={{0,8},{8,16},{16,24},{24,28},{28,20},{20,12},{12,4},{4,0},{1,9},{9... | collective-permute-start | bytes 98312 | tf_op jit(solution)/shard_map/ppermute | solution.py:96
  282.5 12.2 %collective-permute-start.46 = (bf16[1024,128]{1,0:T(8,128)(2,1)S(1)}, bf16[1024,128]{1,0:T(8,128)(2,1)S(1)}, u32[]{:S(2)}, u32[]{:S(2)}) collective-permute-start(bf16[1024,128]{1,0:T(8,128)(2,1)S(1)} %bitcast.286), channel_id=1, source_target_pairs={{0,2},{1,3},{2,0},{3,1},{4,6},{5,7},{6,4},{7,5},{8,10},{9,11},{10,... | collective-permute-start | bytes 786440 | tf_op jit(solution)/shard_map/ppermute | solution.py:32
  283.6 14.8 %collective-permute-start.59 = (bf16[816,128]{1,0:T(8,128)(2,1)S(1)}, bf16[816,128]{1,0:T(8,128)(2,1)S(1)}, u32[]{:S(2)}, u32[]{:S(2)}) collective-permute-start(bf16[816,128]{1,0:T(8,128)(2,1)S(1)} %copy-done.81), channel_id=1, source_target_pairs={{0,3},{1,2},{2,1},{3,0},{4,7},{5,6},{6,5},{7,4},{8,11},{9,10},{10,... | collective-permute-start | bytes 626696 | tf_op jit(solution)/shard_map/ppermute | solution.py:32
  289.1 11.9 %collective-permute-start.45 = (bf16[1024,128]{1,0:T(8,128)(2,1)S(1)}, bf16[1024,128]{1,0:T(8,128)(2,1)S(1)}, u32[]{:S(2)}, u32[]{:S(2)}) collective-permute-start(bf16[1024,128]{1,0:T(8,128)(2,1)S(1)} %bitcast.287), channel_id=1, source_target_pairs={{0,1},{1,0},{2,3},{3,2},{4,5},{5,4},{6,7},{7,6},{8,9},{9,8},{10,11... | collective-permute-start | bytes 786440 | tf_op jit(solution)/shard_map/ppermute | solution.py:32
  301.0 10.0 %collective-permute-start.51 = (bf16[512,512]{1,0:T(8,128)(2,1)S(1)}, bf16[512,512]{1,0:T(8,128)(2,1)S(1)}, u32[]{:S(2)}, u32[]{:S(2)}) collective-permute-start(bf16[512,512]{1,0:T(8,128)(2,1)S(1)} %copy-done.67), channel_id=1, source_target_pairs={{0,1},{1,0},{2,3},{3,2},{4,5},{5,4},{6,7},{7,6},{8,9},{9,8},{10,11... | collective-permute-start | bytes 1572872 | tf_op jit(solution)/shard_map/ppermute | solution.py:32
  328.0 10.3 %collective-permute-start.37 = (bf16[816,128]{1,0:T(8,128)(2,1)}, bf16[816,128]{1,0:T(8,128)(2,1)}, u32[]{:S(2)}, u32[]{:S(2)}) collective-permute-start(bf16[816,128]{1,0:T(8,128)(2,1)} %get-tuple-element.420), channel_id=1, source_target_pairs={{0,3},{1,2},{2,1},{3,0},{4,7},{5,6},{6,5},{7,4},{8,11},{9,10},{10,... | collective-permute-start | bytes 626696 | tf_op jit(solution)/shard_map/ppermute | solution.py:32
  332.7 11.2 %collective-permute-start.33 = (bf16[816,128]{1,0:T(8,128)(2,1)S(1)}, bf16[816,128]{1,0:T(8,128)(2,1)S(1)}, u32[]{:S(2)}, u32[]{:S(2)}) collective-permute-start(bf16[816,128]{1,0:T(8,128)(2,1)S(1)} %get-tuple-element.424), channel_id=1, source_target_pairs={{0,2},{1,3},{2,0},{3,1},{4,6},{5,7},{6,4},{7,5},{8,10},{9,11},{10,... | collective-permute-start | bytes 626696 | tf_op jit(solution)/shard_map/ppermute | solution.py:32
  334.1 12.3 %collective-permute-start.34 = (bf16[816,128]{1,0:T(8,128)(2,1)S(1)}, bf16[816,128]{1,0:T(8,128)(2,1)S(1)}, u32[]{:S(2)}, u32[]{:S(2)}) collective-permute-start(bf16[816,128]{1,0:T(8,128)(2,1)S(1)} %get-tuple-element.423), channel_id=1, source_target_pairs={{0,3},{1,2},{2,1},{3,0},{4,7},{5,6},{6,5},{7,4},{8,11},{9,10},{10,... | collective-permute-start | bytes 626696 | tf_op jit(solution)/shard_map/ppermute | solution.py:32
  400.5 10.0 %collective-permute-start.62 = (bf16[816,128]{1,0:T(8,128)(2,1)S(1)}, bf16[816,128]{1,0:T(8,128)(2,1)S(1)}, u32[]{:S(2)}, u32[]{:S(2)}) collective-permute-start(bf16[816,128]{1,0:T(8,128)(2,1)S(1)} %get-tuple-element.411), channel_id=1, source_target_pairs={{0,3},{1,2},{2,1},{3,0},{4,7},{5,6},{6,5},{7,4},{8,11},{9,10},{10,... | collective-permute-start | bytes 626696 | tf_op jit(solution)/shard_map/ppermute | solution.py:32
  402.4 17.8 %collective-permute-start.63 = (bf16[816,128]{1,0:T(8,128)(2,1)}, bf16[816,128]{1,0:T(8,128)(2,1)}, u32[]{:S(2)}, u32[]{:S(2)}) collective-permute-start(bf16[816,128]{1,0:T(8,128)(2,1)} %get-tuple-element.412), channel_id=1, source_target_pairs={{0,1},{1,0},{2,3},{3,2},{4,5},{5,4},{6,7},{7,6},{8,9},{9,8},{10,11... | collective-permute-start | bytes 626696 | tf_op jit(solution)/shard_map/ppermute | solution.py:32
  403.1 17.1 %collective-permute-start.64 = (bf16[816,128]{1,0:T(8,128)(2,1)}, bf16[816,128]{1,0:T(8,128)(2,1)}, u32[]{:S(2)}, u32[]{:S(2)}) collective-permute-start(bf16[816,128]{1,0:T(8,128)(2,1)} %get-tuple-element.329), channel_id=1, source_target_pairs={{0,2},{1,3},{2,0},{3,1},{4,6},{5,7},{6,4},{7,5},{8,10},{9,11},{10,... | collective-permute-start | bytes 626696 | tf_op jit(solution)/shard_map/ppermute | solution.py:32
  407.8 13.0 %collective-permute-start.65 = (bf16[816,128]{1,0:T(8,128)(2,1)}, bf16[816,128]{1,0:T(8,128)(2,1)}, u32[]{:S(2)}, u32[]{:S(2)}) collective-permute-start(bf16[816,128]{1,0:T(8,128)(2,1)} %get-tuple-element.413), channel_id=1, source_target_pairs={{0,3},{1,2},{2,1},{3,0},{4,7},{5,6},{6,5},{7,4},{8,11},{9,10},{10,... | collective-permute-start | bytes 626696 | tf_op jit(solution)/shard_map/ppermute | solution.py:32
  407.8 25.1 %collective-permute-start.86 = (bf16[512,512]{1,0:T(8,128)(2,1)}, bf16[512,512]{1,0:T(8,128)(2,1)}, u32[]{:S(2)}, u32[]{:S(2)}) collective-permute-start(bf16[512,512]{1,0:T(8,128)(2,1)} %get-tuple-element.342), channel_id=1, source_target_pairs={{0,1},{1,0},{2,3},{3,2},{4,5},{5,4},{6,7},{7,6},{8,9},{9,8},{10,11... | collective-permute-start | bytes 1572872 | tf_op jit(solution)/shard_map/ppermute | solution.py:32
  410.6 54.8 %collective-permute-start.85 = (bf16[512,512]{1,0:T(8,128)(2,1)}, bf16[512,512]{1,0:T(8,128)(2,1)}, u32[]{:S(2)}, u32[]{:S(2)}) collective-permute-start(bf16[512,512]{1,0:T(8,128)(2,1)} %get-tuple-element.341), channel_id=1, source_target_pairs={{0,1},{1,0},{2,3},{3,2},{4,5},{5,4},{6,7},{7,6},{8,9},{9,8},{10,11... | collective-permute-start | bytes 1572872 | tf_op jit(solution)/shard_map/ppermute | solution.py:32
  420.2 18.3 %collective-permute-start.89 = (bf16[512,512]{1,0:T(8,128)(2,1)}, bf16[512,512]{1,0:T(8,128)(2,1)}, u32[]{:S(2)}, u32[]{:S(2)}) collective-permute-start(bf16[512,512]{1,0:T(8,128)(2,1)} %get-tuple-element.344), channel_id=1, source_target_pairs={{0,1},{1,0},{2,3},{3,2},{4,5},{5,4},{6,7},{7,6},{8,9},{9,8},{10,11... | collective-permute-start | bytes 1572872 | tf_op jit(solution)/shard_map/ppermute | solution.py:32
  420.2 10.8 %collective-permute-start.83 = (bf16[1024,128]{1,0:T(8,128)(2,1)}, bf16[1024,128]{1,0:T(8,128)(2,1)}, u32[]{:S(2)}, u32[]{:S(2)}) collective-permute-start(bf16[1024,128]{1,0:T(8,128)(2,1)} %get-tuple-element.354), channel_id=1, source_target_pairs={{0,1},{1,0},{2,3},{3,2},{4,5},{5,4},{6,7},{7,6},{8,9},{9,8},{10,11... | collective-permute-start | bytes 786440 | tf_op jit(solution)/shard_map/ppermute | solution.py:32
  420.7 21.3 %collective-permute-start.82 = (bf16[1024,128]{1,0:T(8,128)(2,1)}, bf16[1024,128]{1,0:T(8,128)(2,1)}, u32[]{:S(2)}, u32[]{:S(2)}) collective-permute-start(bf16[1024,128]{1,0:T(8,128)(2,1)} %get-tuple-element.353), channel_id=1, source_target_pairs={{0,1},{1,0},{2,3},{3,2},{4,5},{5,4},{6,7},{7,6},{8,9},{9,8},{10,11... | collective-permute-start | bytes 786440 | tf_op jit(solution)/shard_map/ppermute | solution.py:32
  436.8 28.6 %collective-permute-start.87 = (bf16[512,512]{1,0:T(8,128)(2,1)}, bf16[512,512]{1,0:T(8,128)(2,1)}, u32[]{:S(2)}, u32[]{:S(2)}) collective-permute-start(bf16[512,512]{1,0:T(8,128)(2,1)} %add_convert_fusion.11), channel_id=1, source_target_pairs={{0,2},{1,3},{2,0},{3,1},{4,6},{5,7},{6,4},{7,5},{8,10},{9,11},{10,... | collective-permute-start | bytes 1572872 | tf_op jit(solution)/shard_map/ppermute | solution.py:32
  438.5 25.5 %collective-permute-start.67 = (f32[476,256]{1,0:T(8,128)}, f32[476,256]{1,0:T(8,128)}, u32[]{:S(2)}, u32[]{:S(2)}) collective-permute-start(f32[476,256]{1,0:T(8,128)} %maximum_add_fusion), channel_id=1, source_target_pairs={{0,2},{1,3},{2,0},{3,1},{4,6},{5,7},{6,4},{7,5},{8,10},{9,11},{10,... | collective-permute-start | bytes 1462280 | tf_op jit(solution)/shard_map/ppermute | solution.py:32
  442.0 26.6 %collective-permute-start.88 = (bf16[512,512]{1,0:T(8,128)(2,1)}, bf16[512,512]{1,0:T(8,128)(2,1)}, u32[]{:S(2)}, u32[]{:S(2)}) collective-permute-start(bf16[512,512]{1,0:T(8,128)(2,1)} %get-tuple-element.343), channel_id=1, source_target_pairs={{0,1},{1,0},{2,3},{3,2},{4,5},{5,4},{6,7},{7,6},{8,9},{9,8},{10,11... | collective-permute-start | bytes 1572872 | tf_op jit(solution)/shard_map/ppermute | solution.py:32
  442.2 32.1 %collective-permute-start.90 = (bf16[512,512]{1,0:T(8,128)(2,1)}, bf16[512,512]{1,0:T(8,128)(2,1)}, u32[]{:S(2)}, u32[]{:S(2)}) collective-permute-start(bf16[512,512]{1,0:T(8,128)(2,1)} %add_convert_fusion.9), channel_id=1, source_target_pairs={{0,2},{1,3},{2,0},{3,1},{4,6},{5,7},{6,4},{7,5},{8,10},{9,11},{10,... | collective-permute-start | bytes 1572872 | tf_op jit(solution)/shard_map/ppermute | solution.py:32
  445.4 385.2 %reduce-scatter.17.cloned.1.call-start = ((), (), s32[]{:S(2)}) async-start(), calls=%async_computation.15 | async-start | bytes 1179648 | tf_op jit(solution)/shard_map/reduce_scatter | solution.py:112
  465.3 11.9 %collective-permute-start.68 = (f32[476,256]{1,0:T(8,128)S(1)}, f32[476,256]{1,0:T(8,128)S(1)}, u32[]{:S(2)}, u32[]{:S(2)}) collective-permute-start(f32[476,256]{1,0:T(8,128)S(1)} %add.1167), channel_id=1, source_target_pairs={{0,1},{1,0},{2,3},{3,2},{4,5},{5,4},{6,7},{7,6},{8,9},{9,8},{10,11... | collective-permute-start | bytes 1462280 | tf_op jit(solution)/shard_map/ppermute | solution.py:32
  477.1 405.3 %reduce-scatter.9.cloned.1.call-start = ((), (), s32[]{:S(2)}) async-start(), calls=%async_computation.11 | async-start | bytes 1769472 | tf_op jit(solution)/shard_map/reduce_scatter | solution.py:112
  486.8 26.1 %collective-permute-start.72 = (bf16[476,128]{1,0:T(8,128)(2,1)S(1)}, bf16[476,128]{1,0:T(8,128)(2,1)S(1)}, u32[]{:S(2)}, u32[]{:S(2)}) collective-permute-start(bf16[476,128]{1,0:T(8,128)(2,1)S(1)} %collective-permute-done.70), channel_id=1, source_target_pairs={{8,0},{16,8},{24,16},{28,24},{20,28},{12,20},{4,12},{0,4},{9,1},{1... | collective-permute-start | bytes 365576 | tf_op jit(solution)/shard_map/ppermute | solution.py:99
  490.8 23.4 %collective-permute-start.73 = (bf16[476,128]{1,0:T(8,128)(2,1)S(1)}, bf16[476,128]{1,0:T(8,128)(2,1)S(1)}, u32[]{:S(2)}, u32[]{:S(2)}) collective-permute-start(bf16[476,128]{1,0:T(8,128)(2,1)S(1)} %collective-permute-done.71), channel_id=1, source_target_pairs={{0,8},{8,16},{16,24},{24,28},{28,20},{20,12},{12,4},{4,0},{1,9},{9... | collective-permute-start | bytes 365576 | tf_op jit(solution)/shard_map/ppermute | solution.py:96
  512.9 38.2 %collective-permute-start.74 = (bf16[476,128]{1,0:T(8,128)(2,1)S(1)}, bf16[476,128]{1,0:T(8,128)(2,1)S(1)}, u32[]{:S(2)}, u32[]{:S(2)}) collective-permute-start(bf16[476,128]{1,0:T(8,128)(2,1)S(1)} %collective-permute-done.72), channel_id=1, source_target_pairs={{8,0},{16,8},{24,16},{28,24},{20,28},{12,20},{4,12},{0,4},{9,1},{1... | collective-permute-start | bytes 365576 | tf_op jit(solution)/shard_map/ppermute | solution.py:99
  514.2 49.9 %collective-permute-start.75 = (bf16[476,128]{1,0:T(8,128)(2,1)S(1)}, bf16[476,128]{1,0:T(8,128)(2,1)S(1)}, u32[]{:S(2)}, u32[]{:S(2)}) collective-permute-start(bf16[476,128]{1,0:T(8,128)(2,1)S(1)} %collective-permute-done.73), channel_id=1, source_target_pairs={{0,8},{8,16},{16,24},{24,28},{28,20},{20,12},{12,4},{4,0},{1,9},{9... | collective-permute-start | bytes 365576 | tf_op jit(solution)/shard_map/ppermute | solution.py:96
  517.6 380.4 %reduce-scatter.13.cloned.1.call-start = ((), (), s32[]{:S(2)}) async-start(), calls=%async_computation.13 | async-start | bytes 2359296 | tf_op jit(solution)/shard_map/reduce_scatter | solution.py:112
  704.3 14.4 %collective-permute-start.77 = (bf16[8,476,128]{2,0,1:T(8,128)(2,1)}, bf16[8,476,128]{2,0,1:T(8,128)(2,1)S(1)}, u32[]{:S(2)}, u32[]{:S(2)}) collective-permute-start(bf16[8,476,128]{2,0,1:T(8,128)(2,1)} %select_convert_fusion), channel_id=1, source_target_pairs={{0,1},{1,0},{2,3},{3,2},{4,5},{5,4},{6,7},{7,6},{8,9},{9,8},{10,11... | collective-permute-start | bytes 2924552 | tf_op jit(solution)/shard_map/ppermute | solution.py:32
  717.9 62.1 %collective-permute-start.76 = (bf16[8,476,128]{2,0,1:T(8,128)(2,1)}, bf16[8,476,128]{2,0,1:T(8,128)(2,1)}, u32[]{:S(2)}, u32[]{:S(2)}) collective-permute-start(bf16[8,476,128]{2,0,1:T(8,128)(2,1)} %get-tuple-element.319), channel_id=1, source_target_pairs={{0,1},{1,0},{2,3},{3,2},{4,5},{5,4},{6,7},{7,6},{8,9},{9,8},{10,11... | collective-permute-start | bytes 2924552 | tf_op jit(solution)/shard_map/ppermute | solution.py:32
  721.6 58.4 %collective-permute-start.78 = (bf16[8,476,128]{2,0,1:T(8,128)(2,1)}, bf16[8,476,128]{2,0,1:T(8,128)(2,1)S(1)}, u32[]{:S(2)}, u32[]{:S(2)}) collective-permute-start(bf16[8,476,128]{2,0,1:T(8,128)(2,1)} %add_convert_fusion.2), channel_id=1, source_target_pairs={{0,2},{1,3},{2,0},{3,1},{4,6},{5,7},{6,4},{7,5},{8,10},{9,11},{10,... | collective-permute-start | bytes 2924552 | tf_op jit(solution)/shard_map/ppermute | solution.py:32
  783.5 29.5 %all-to-all-start.1 = ((bf16[8,476,128]{2,1,0:T(8,128)(2,1)}), bf16[8,476,128]{2,1,0:T(8,128)(2,1)}, u32[]{:S(2)}, u32[]{:S(2)}) async-start(bf16[8,476,128]{2,1,0:T(8,128)(2,1)} %copy.120), calls=%async_computation.1 | async-start | bytes 1966080 | tf_op jit(solution)/shard_map/all_to_all | solution.py:107
  788.4 136.0 %reduce-scatter.7.cloned.1.call-start = ((), (), s32[]{:S(2)}) async-start(), calls=%async_computation.10 | async-start | bytes 1769472 | tf_op jit(solution)/shard_map/reduce_scatter | solution.py:112
  818.8 135.0 %reduce-scatter.11.cloned.1.call-start = ((), (), s32[]{:S(2)}) async-start(), calls=%async_computation.12 | async-start | bytes 2359296 | tf_op jit(solution)/shard_map/reduce_scatter | solution.py:112
  836.0 48.1 %collective-permute-start.93 = (bf16[128,512]{1,0:T(8,128)(2,1)}, bf16[128,512]{1,0:T(8,128)(2,1)S(1)}, u32[]{:S(2)}, u32[]{:S(2)}) collective-permute-start(bf16[128,512]{1,0:T(8,128)(2,1)} %collective-permute-done.91), channel_id=1, source_target_pairs={{0,8},{8,16},{16,24},{24,28},{28,20},{20,12},{12,4},{4,0},{1,9},{9... | collective-permute-start | bytes 393224 | tf_op jit(solution)/shard_map/ppermute | solution.py:96
  838.5 46.0 %collective-permute-start.94 = (bf16[128,512]{1,0:T(8,128)(2,1)}, bf16[128,512]{1,0:T(8,128)(2,1)S(1)}, u32[]{:S(2)}, u32[]{:S(2)}) collective-permute-start(bf16[128,512]{1,0:T(8,128)(2,1)} %collective-permute-done.92), channel_id=1, source_target_pairs={{8,0},{16,8},{24,16},{28,24},{20,28},{12,20},{4,12},{0,4},{9,1},{1... | collective-permute-start | bytes 393224 | tf_op jit(solution)/shard_map/ppermute | solution.py:99
  880.6 9.8 %collective-permute-start.80 = (bf16[3264,128]{1,0:T(8,128)(2,1)S(1)}, bf16[3264,128]{1,0:T(8,128)(2,1)S(1)}, u32[]{:S(2)}, u32[]{:S(2)}) collective-permute-start(bf16[3264,128]{1,0:T(8,128)(2,1)S(1)} %get-tuple-element.340), channel_id=1, source_target_pairs={{0,1},{1,0},{2,3},{3,2},{4,5},{5,4},{6,7},{7,6},{8,9},{9,8},{10,11... | collective-permute-start | bytes 2506760 | tf_op jit(solution)/shard_map/ppermute | solution.py:32
  884.5 11.1 %collective-permute-start.96 = (bf16[128,512]{1,0:T(8,128)(2,1)S(1)}, bf16[128,512]{1,0:T(8,128)(2,1)S(1)}, u32[]{:S(2)}, u32[]{:S(2)}) collective-permute-start(bf16[128,512]{1,0:T(8,128)(2,1)S(1)} %collective-permute-done.94), channel_id=1, source_target_pairs={{8,0},{16,8},{24,16},{28,24},{20,28},{12,20},{4,12},{0,4},{9,1},{1... | collective-permute-start | bytes 393224 | tf_op jit(solution)/shard_map/ppermute | solution.py:99
  894.7 21.4 %collective-permute-start.81 = (bf16[3264,128]{1,0:T(8,128)(2,1)}, bf16[3264,128]{1,0:T(8,128)(2,1)}, u32[]{:S(2)}, u32[]{:S(2)}) collective-permute-start(bf16[3264,128]{1,0:T(8,128)(2,1)} %add_convert_fusion.3), channel_id=1, source_target_pairs={{0,2},{1,3},{2,0},{3,1},{4,6},{5,7},{6,4},{7,5},{8,10},{9,11},{10,... | collective-permute-start | bytes 2506760 | tf_op jit(solution)/shard_map/ppermute | solution.py:32
  (150 other events, 1375.7 us)
Sparse Core Ops, SparseCore 0:
  14.0 51.2 all-gather.2
  109.0 53.3 all-gather.4
  445.5 60.9 reduce-scatter.14
  510.3 62.6 reduce-scatter.16
  577.2 64.8 reduce-scatter.8
  710.8 69.0 reduce-scatter.12
  818.9 64.3 reduce-scatter.6
  887.2 66.5 reduce-scatter.10
where the time goes:
time: 975 us; the launch traced here: 963 us
  local copies, waits for them, and re-layouts  257 us (26%)
  waiting for transfers between devices  227 us (23%)
  other arithmetic  151 us (15%)
  matrix products  150 us (15%)
  starting transfers between devices  89.1 us (9%)
  blocking collectives  53.8 us (6%)
  between operations  35.3 us (4%)
    ppermute x56, waiting for transfers between devices, swap(): return lax.ppermute(value, 'tensor', [(i, i ^ mask) for i in range(4)])  81.5 us
    dot_general x9, matrix products, matmul(): return jnp.dot(left, right, preferred_element_type=F32)  65 us
    psum x1, blocking collectives, body(): sums = own_lanes(lax.psum(sums, ('dp', 'tensor')))  53.8 us
    ppermute x18, waiting for transfers between devices, ring_gather(): behind = lax.ppermute(behind, 'dp', down)  52.4 us
    dot_general x9, matrix products, against(): lax.dot_general(left, right, (((1,), (1,)), ((), ())), preferred_element_...  50.7 us
    ppermute x24, waiting for transfers between devices, ring_gather(): ahead = lax.ppermute(ahead, 'dp', up)  48.7 us
    scatter-add x15, other arithmetic, iso_backward(): total = total.at[j:j + span_len].add(spread[:, :, j * D:(j + 1) * D])  39.3 us
    unnamed x223, local copies, waits for them, and re-layouts  35.1 us
  transfers between devices with their start and end apart: 108, of which 41 were waited for; matrix products, arithmetic and copies ran while one was open for 50% of the time, Pallas kernels for 0%

commit v1 on v0

--- a/solution.py
+++ b/solution.py
@@ -340,7 +340,7 @@
             grad_last_bias,
         ]
     )
-    sums = own_lanes(lax.psum(sums, ("dp", "tensor")))
+    sums = own_lanes(lax.psum(lax.psum(sums, axis_name="dp"), axis_name="tensor"))
     return (
         series_out,
         grad_input,

time: 975 us -> 967 us (level)
    psum x1 -> x2, blocking collectives: 53.8 us -> 46.4 us  [the longest x1 35.8 us: body(): lax.psum(sums, axis_name='dp')]
  transfers between devices with their start and end apart: 108 -> 108, of which waited for: 41 -> 42; matrix products, arithmetic and copies ran while one was open for 50% -> 50% of each run, Pallas kernels for 0% -> 0%
where the time goes in v1:
time: 967 us; the launch traced here: 955 us
  local copies, waits for them, and re-layouts  257 us (27%)
  waiting for transfers between devices  226 us (23%)
  other arithmetic  151 us (16%)
  matrix products  150 us (16%)
  starting transfers between devices  89.2 us (9%)
  blocking collectives  46.4 us (5%)
  between operations  35.3 us (4%)
    ppermute x56, waiting for transfers between devices, swap(): return lax.ppermute(value, 'tensor', [(i, i ^ mask) for i in range(4)])  81.3 us
    dot_general x9, matrix products, matmul(): return jnp.dot(left, right, preferred_element_type=F32)  65.1 us
    ppermute x18, waiting for transfers between devices, ring_gather(): behind = lax.ppermute(behind, 'dp', down)  52.9 us
    dot_general x9, matrix products, against(): lax.dot_general(left, right, (((1,), (1,)), ((), ())), preferred_element_...  50.7 us
    ppermute x24, waiting for transfers between devices, ring_gather(): ahead = lax.ppermute(ahead, 'dp', up)  48.1 us
    scatter-add x15, other arithmetic, iso_backward(): total = total.at[j:j + span_len].add(spread[:, :, j * D:(j + 1) * D])  39.3 us
    psum x1, blocking collectives, body(): lax.psum(sums, axis_name='dp')  35.8 us
    unnamed x223, local copies, waits for them, and re-layouts  35.2 us
  transfers between devices with their start and end apart: 108, of which 42 were waited for; matrix products, arithmetic and copies ran while one was open for 50% of the time, Pallas kernels for 0%

profile of v1, /device:TPU:0, one launch (start us, length us, event | category | flops | bytes accessed | tf_op | source)
XLA Modules:
  0.0 954.9 jit_solution(3431091619947604045)
XLA Ops:
  41.1 11.8 %collective-permute-done.11 = bf16[1024,128]{1,0:T(8,128)(2,1)S(1)} collective-permute-done((bf16[1024,128]{1,0:T(8,128)(2,1)S(1)}, bf16[1024,128]{1,0:T(8,128)(2,1)S(1)}, u32[]{:S(2)}, u32[]{:S(2)}) %collective-permute-start.11) | collective-permute-done | bytes 262176 | tf_op jit(solution)/shard_map/ppermute | solution.py:99
  55.0 6.5 collective-permute-done.6
  80.7 4.2 collective-permute-done.16
  87.6 5.0 reshape.927
  95.9 3.6 convolution_tanh_fusion.2
  101.8 4.3 collective-permute-done.17
  109.8 3.5 collective-permute-done.18
  113.4 3.6 collective-permute-done.19
  120.5 10.6 %collective-permute-done.21 = bf16[476,256]{1,0:T(8,128)(2,1)S(1)} collective-permute-done((bf16[476,256]{1,0:T(8,128)(2,1)S(1)}, bf16[476,256]{1,0:T(8,128)(2,1)S(1)}, u32[]{:S(2)}, u32[]{:S(2)}) %collective-permute-start.21) | collective-permute-done | bytes 243744 | tf_op jit(solution)/shard_map/ppermute | solution.py:99
  133.2 5.8 collective-permute-done.23
  172.7 21.0 %fusion.53 = bf16[8,4,68,128]{3,2,1,0:T(8,128)(2,1)S(1)} fusion(bf16[68,8,4,4608]{3,0,2,1:T(8,128)(2,1)S(1)} %bitcast.258, bf16[4608,128]{1,0:T(8,128)(2,1)} %constant_dynamic-update-slice_fusion), kind=kOutput, calls=%fused_computation.173 | convolution fusion | flops 2567192576 | bytes 21790720 | tf_op jit(solution)/shard_map/dot_general | solution.py:20
  212.5 22.6 %dot_general.101 = bf16[51,8,4,4096]{3,2,1,0:T(4,128)(2,1)} reshape(bf16[51,32,4096]{2,1,0:T(8,128)(2,1)} %fusion.38) | data formatting | bytes 26738688 | tf_op jit(solution)/shard_map/dot_general | solution.py:20
  235.1 10.3 %fusion.54 = bf16[8,4,51,128]{3,1,0,2:T(4,128)(2,1)S(1)} fusion(bf16[51,8,4,4096]{3,2,1,0:T(4,128)(2,1)} %dot_general.101, bf16[4096,128]{1,0:T(8,128)(2,1)} %constant_dynamic-update-slice_fusion.2), kind=kOutput, calls=%fused_computation.174 | convolution fusion | flops 1711484928 | bytes 14835712 | tf_op jit(solution)/shard_map/dot_general | solution.py:20
  246.7 4.5 all-to-all-start
  253.3 13.6 %collective-permute-done.42 = bf16[128,128]{1,0:T(8,128)(2,1)S(1)} collective-permute-done((bf16[128,128]{1,0:T(8,128)(2,1)S(1)}, bf16[128,128]{1,0:T(8,128)(2,1)S(1)}, u32[]{:S(2)}, u32[]{:S(2)}) %collective-permute-start.42) | collective-permute-done | bytes 32800 | tf_op jit(solution)/shard_map/ppermute | solution.py:96
  266.9 8.5 collective-permute-done.43
  284.2 4.9 collective-permute-done.58
  289.1 5.6 collective-permute-done.46
  294.7 3.7 collective-permute-done.59
  307.3 3.7 collective-permute-done.27
  319.3 3.5 fusion.116
  339.8 4.0 collective-permute-done.33
  350.4 19.6 %multiply_convert_fusion = (bf16[816,2048]{1,0:T(8,128)(2,1)S(1)}, f32[816,2048]{1,0:T(8,128)}, f32[816,2048]{1,0:T(8,128)}) fusion(bf16[512,512]{1,0:T(8,128)(2,1)S(1)} %copy-done.71, bf16[512,512]{1,0:T(8,128)(2,1)S(1)} %copy-done.70, bf16[512,512]{1,0:T(8,128)(2,1)S(1)} %copy-done.69, bf16[512,512]{1,0:T(8,128)(2,1)S(1)} %copy-done.68, ...), kind=kOutput, calls=%fused_computation.28 | convolution fusion | flops 1830379520 | bytes 20490624 | tf_op jit(solution)/shard_map/dot_general | solution.py:20
  373.7 7.2 add_convert_fusion
  445.7 18.4 %collective-permute-done.67 = f32[476,256]{1,0:T(8,128)} collective-permute-done((f32[476,256]{1,0:T(8,128)}, f32[476,256]{1,0:T(8,128)}, u32[]{:S(2)}, u32[]{:S(2)}) %collective-permute-start.67) | collective-permute-done | bytes 487456 | tf_op jit(solution)/shard_map/ppermute | solution.py:32
  468.9 5.5 collective-permute-done.90
  492.0 20.9 %copy.121 = bf16[68,32,4608]{2,1,0:T(8,128)(2,1)} copy(bf16[68,32,4608]{2,0,1:T(8,128)(2,1)} %copy-done.11) | data formatting | bytes 40108032 | tf_op jit(solution)/shard_map/concatenate | solution.py:150
  518.0 6.4 dynamic_update_slice.196
  524.9 6.4 dynamic_update_slice.197
  531.3 6.4 dynamic_update_slice.198
  538.1 6.4 dynamic_update_slice.199
  544.5 6.4 dynamic_update_slice.200
  551.3 6.4 dynamic_update_slice.201
  557.7 6.4 dynamic_update_slice.202
  564.3 6.4 dynamic_update_slice.203
  571.1 17.4 %fusion.56 = f32[68,32,4608]{2,1,0:T(8,128)} fusion(bf16[68,32,128]{2,1,0:T(8,128)(2,1)S(1)} %bitcast.272, bf16[4608,128]{1,0:T(8,128)(2,1)} %constant_dynamic-update-slice_fusion), kind=kOutput, calls=%fused_computation.176 | convolution fusion | flops 2566914048 | bytes 41844736 | tf_op jit(solution)/shard_map/dot_general | solution.py:28
  591.7 3.5 fusion.13
  595.1 3.5 fusion.12
  602.1 3.5 fusion.10
  605.6 3.5 fusion.9
  619.4 5.6 copy.116
  625.0 4.9 broadcast_in_dim.247
  629.8 22.2 %dynamic_update_slice.204 = f32[144,32,512]{2,0,1:T(8,128)} dynamic-update-slice(f32[144,32,512]{2,0,1:T(8,128)} %broadcast_in_dim.247, f32[76,32,512]{2,0,1:T(8,128)} %copy.116, s32[]{:T(128)S(6)} %select_n.1414, s32[]{:T(128)} %constant.1016.clone.1, s32[]{:T(128)} %constant.1016.clone.1) | dynamic-update-slice | bytes 9961476 | tf_op jit(solution)/shard_map/dynamic_update_slice | solution.py:171
  655.2 4.6 copy.117
  660.0 12.2 %fusion.61 = f32[51,32,4096]{2,1,0:T(8,128)} fusion(bf16[51,32,128]{2,1,0:T(8,128)(2,1)S(1)} %bitcast.274, bf16[4096,128]{1,0:T(8,128)(2,1)} %constant_dynamic-update-slice_fusion.2), kind=kOutput, calls=%fused_computation.185 | convolution fusion | flops 1711276032 | bytes 28205056 | tf_op jit(solution)/shard_map/dot_general | solution.py:28
  677.8 3.5 fusion.19
  697.6 3.9 select_convert_fusion.1
  725.8 35.8 %psum.14 = f32[6,512]{1,0:T(8,128)S(1)} all-reduce(f32[6,512]{1,0:T(8,128)S(1)} %stack.49), channel_id=1, replica_groups=mesh['dp'=8,'tensor'=4] {'dp'}, use_global_device_ids=true, to_apply=%region_38.39 | all-reduce | flops 3072 | bytes 24576 | tf_op jit(solution)/shard_map/psum | solution.py:343
  761.6 10.6 %psum.15 = f32[6,512]{1,0:T(8,128)S(1)} all-reduce(f32[6,512]{1,0:T(8,128)S(1)} %psum.14), channel_id=1, replica_groups=mesh['dp'=8,'tensor'=4] {'tensor'}, use_global_device_ids=true, to_apply=%region_39.40 | all-reduce | flops 3072 | bytes 24576 | tf_op jit(solution)/shard_map/psum | solution.py:343
  776.2 4.2 all-to-all-start.1
  780.5 7.1 fusion.119
  788.9 15.4 %all-to-all-done.1 = bf16[8,476,128]{2,1,0:T(8,128)(2,1)} async-done(((bf16[8,476,128]{2,1,0:T(8,128)(2,1)}), bf16[8,476,128]{2,1,0:T(8,128)(2,1)}, u32[]{:S(2)}, u32[]{:S(2)}) %all-to-all-start.1) | async-done | bytes 974880 | tf_op jit(solution)/shard_map/all_to_all | solution.py:107
  810.2 10.2 %fusion.118 = f32[4608,128]{1,0:T(8,128)S(1)} fusion(bf16[2176,4608]{1,0:T(8,128)(2,1)} %bitcast.259, bf16[2176,128]{1,0:T(8,128)(2,1)} %bitcast.273), kind=kOutput, calls=%fused_computation.513 | convolution fusion | flops 2566914048 | bytes 22970368 | tf_op jit(solution)/shard_map/dot_general | solution.py:24
  832.0 3.9 fusion.89
  835.9 8.4 reshape.948
  844.2 3.8 fusion.86
  848.1 7.9 reshape.947
  856.0 9.4 add.1217
  868.1 4.3 select_convert_fusion.3
  878.1 4.1 collective-permute-done.95
  882.2 4.2 add_convert_fusion.3
  891.9 15.9 %collective-permute-done.81 = bf16[3264,128]{1,0:T(8,128)(2,1)} collective-permute-done((bf16[3264,128]{1,0:T(8,128)(2,1)}, bf16[3264,128]{1,0:T(8,128)(2,1)}, u32[]{:S(2)}, u32[]{:S(2)}) %collective-permute-start.81) | collective-permute-done | bytes 835616 | tf_op jit(solution)/shard_map/ppermute | solution.py:32
  907.9 8.2 add_add_fusion
  917.8 28.0 %reduce-scatter.11.cloned.1.call-done = bf16[1024,128]{1,0:T(8,128)(2,1)} async-done(((bf16[8192,128]{1,0:T(8,128)(2,1)}), bf16[1024,128]{1,0:T(8,128)(2,1)}) %reduce-scatter.11.cloned.1.call-update) | async-done | bytes 262160 | tf_op jit(solution)/shard_map/reduce_scatter | solution.py:112
  (647 shorter events, 362.3 us)
Async XLA Ops:
  7.2 306.6 %all-gather.3.cloned.1.call-start = ((), (), s32[]{:S(2)}) async-start(), calls=%async_computation.8 | async-start | bytes 1769472 | tf_op jit(solution)/shard_map/all_gather | solution.py:210
  7.2 29.3 %collective-permute-start.3 = (bf16[768,128]{1,0:T(8,128)(2,1)}, bf16[768,128]{1,0:T(8,128)(2,1)}, u32[]{:S(2)}, u32[]{:S(2)}) collective-permute-start(bf16[768,128]{1,0:T(8,128)(2,1)} %param.66), channel_id=1, source_target_pairs={{0,8},{8,16},{16,24},{24,28},{28,20},{20,12},{12,4},{4,0},{1,9},{9... | collective-permute-start | bytes 589832 | tf_op jit(solution)/shard_map/ppermute | solution.py:96
  10.3 27.7 %collective-permute-start.4 = (bf16[768,128]{1,0:T(8,128)(2,1)}, bf16[768,128]{1,0:T(8,128)(2,1)}, u32[]{:S(2)}, u32[]{:S(2)}) collective-permute-start(bf16[768,128]{1,0:T(8,128)(2,1)} %param.66), channel_id=1, source_target_pairs={{8,0},{16,8},{24,16},{28,24},{20,28},{12,20},{4,12},{0,4},{9,1},{1... | collective-permute-start | bytes 589832 | tf_op jit(solution)/shard_map/ppermute | solution.py:99
  10.3 66.1 %collective-permute-start.1 = (bf16[3264,128]{1,0:T(8,128)(2,1)}, bf16[3264,128]{1,0:T(8,128)(2,1)S(1)}, u32[]{:S(2)}, u32[]{:S(2)}) collective-permute-start(bf16[3264,128]{1,0:T(8,128)(2,1)} %param.64), channel_id=1, source_target_pairs={{0,2},{1,3},{2,0},{3,1},{4,6},{5,7},{6,4},{7,5},{8,10},{9,11},{10,... | collective-permute-start | bytes 2506760 | tf_op jit(solution)/shard_map/ppermute | solution.py:32
  12.3 72.7 %collective-permute-start = (bf16[3264,128]{1,0:T(8,128)(2,1)}, bf16[3264,128]{1,0:T(8,128)(2,1)}, u32[]{:S(2)}, u32[]{:S(2)}) collective-permute-start(bf16[3264,128]{1,0:T(8,128)(2,1)} %param.64), channel_id=1, source_target_pairs={{0,1},{1,0},{2,3},{3,2},{4,5},{5,4},{6,7},{7,6},{8,9},{9,8},{10,11... | collective-permute-start | bytes 2506760 | tf_op jit(solution)/shard_map/ppermute | solution.py:32
  12.3 28.3 %collective-permute-start.10 = (bf16[1024,128]{1,0:T(8,128)(2,1)}, bf16[1024,128]{1,0:T(8,128)(2,1)S(1)}, u32[]{:S(2)}, u32[]{:S(2)}) collective-permute-start(bf16[1024,128]{1,0:T(8,128)(2,1)} %param.69), channel_id=1, source_target_pairs={{0,8},{8,16},{16,24},{24,28},{28,20},{20,12},{12,4},{4,0},{1,9},{9... | collective-permute-start | bytes 786440 | tf_op jit(solution)/shard_map/ppermute | solution.py:96
  13.9 305.4 %all-gather.5.cloned.1.call-start = ((), (), s32[]{:S(2)}) async-start(), calls=%async_computation.9 | async-start | bytes 2359296 | tf_op jit(solution)/shard_map/all_gather | solution.py:211
  36.5 16.4 %collective-permute-start.11 = (bf16[1024,128]{1,0:T(8,128)(2,1)S(1)}, bf16[1024,128]{1,0:T(8,128)(2,1)S(1)}, u32[]{:S(2)}, u32[]{:S(2)}) collective-permute-start(bf16[1024,128]{1,0:T(8,128)(2,1)S(1)} %copy-done.76), channel_id=1, source_target_pairs={{8,0},{16,8},{24,16},{28,24},{20,28},{12,20},{4,12},{0,4},{9,1},{1... | collective-permute-start | bytes 786440 | tf_op jit(solution)/shard_map/ppermute | solution.py:99
  38.0 15.2 %collective-permute-start.5 = (bf16[768,128]{1,0:T(8,128)(2,1)}, bf16[768,128]{1,0:T(8,128)(2,1)S(1)}, u32[]{:S(2)}, u32[]{:S(2)}) collective-permute-start(bf16[768,128]{1,0:T(8,128)(2,1)} %collective-permute-done.3), channel_id=1, source_target_pairs={{0,8},{8,16},{16,24},{24,28},{28,20},{20,12},{12,4},{4,0},{1,9},{9... | collective-permute-start | bytes 589832 | tf_op jit(solution)/shard_map/ppermute | solution.py:96
  40.6 20.9 %collective-permute-start.6 = (bf16[768,128]{1,0:T(8,128)(2,1)}, bf16[768,128]{1,0:T(8,128)(2,1)S(1)}, u32[]{:S(2)}, u32[]{:S(2)}) collective-permute-start(bf16[768,128]{1,0:T(8,128)(2,1)} %collective-permute-done.4), channel_id=1, source_target_pairs={{8,0},{16,8},{24,16},{28,24},{20,28},{12,20},{4,12},{0,4},{9,1},{1... | collective-permute-start | bytes 589832 | tf_op jit(solution)/shard_map/ppermute | solution.py:99
  52.9 10.3 %collective-permute-start.12 = (bf16[1024,128]{1,0:T(8,128)(2,1)S(1)}, bf16[1024,128]{1,0:T(8,128)(2,1)S(1)}, u32[]{:S(2)}, u32[]{:S(2)}) collective-permute-start(bf16[1024,128]{1,0:T(8,128)(2,1)S(1)} %collective-permute-done.10), channel_id=1, source_target_pairs={{0,8},{8,16},{16,24},{24,28},{28,20},{20,12},{12,4},{4,0},{1,9},{9... | collective-permute-start | bytes 786440 | tf_op jit(solution)/shard_map/ppermute | solution.py:96
  53.2 14.9 %collective-permute-start.13 = (bf16[1024,128]{1,0:T(8,128)(2,1)S(1)}, bf16[1024,128]{1,0:T(8,128)(2,1)S(1)}, u32[]{:S(2)}, u32[]{:S(2)}) collective-permute-start(bf16[1024,128]{1,0:T(8,128)(2,1)S(1)} %collective-permute-done.11), channel_id=1, source_target_pairs={{8,0},{16,8},{24,16},{28,24},{20,28},{12,20},{4,12},{0,4},{9,1},{1... | collective-permute-start | bytes 786440 | tf_op jit(solution)/shard_map/ppermute | solution.py:99
  106.9 171.4 %collective-permute-start.30 = (f32[6,128]{1,0:T(8,128)S(1)}, f32[6,128]{1,0:T(8,128)S(1)}, u32[]{:S(2)}, u32[]{:S(2)}) collective-permute-start(f32[6,128]{1,0:T(8,128)S(1)} %stack.44), channel_id=1, source_target_pairs={{0,2},{1,3},{2,0},{3,1},{4,6},{5,7},{6,4},{7,5},{8,10},{9,11},{10,... | collective-permute-start | bytes 9224 | tf_op jit(solution)/shard_map/ppermute | solution.py:32
  107.5 173.6 %collective-permute-start.29 = (f32[6,128]{1,0:T(8,128)S(1)}, f32[6,128]{1,0:T(8,128)S(1)}, u32[]{:S(2)}, u32[]{:S(2)}) collective-permute-start(f32[6,128]{1,0:T(8,128)S(1)} %stack.44), channel_id=1, source_target_pairs={{0,1},{1,0},{2,3},{3,2},{4,5},{5,4},{6,7},{7,6},{8,9},{9,8},{10,11... | collective-permute-start | bytes 9224 | tf_op jit(solution)/shard_map/ppermute | solution.py:32
  107.5 41.1 %collective-permute-start.38 = (bf16[128,128]{1,0:T(8,128)(2,1)S(1)}, bf16[128,128]{1,0:T(8,128)(2,1)S(1)}, u32[]{:S(2)}, u32[]{:S(2)}) collective-permute-start(bf16[128,128]{1,0:T(8,128)(2,1)S(1)} %copy-done.84), channel_id=1, source_target_pairs={{0,8},{8,16},{16,24},{24,28},{28,20},{20,12},{12,4},{4,0},{1,9},{9... | collective-permute-start | bytes 98312 | tf_op jit(solution)/shard_map/ppermute | solution.py:96
  117.0 14.0 %collective-permute-start.21 = (bf16[476,256]{1,0:T(8,128)(2,1)S(1)}, bf16[476,256]{1,0:T(8,128)(2,1)S(1)}, u32[]{:S(2)}, u32[]{:S(2)}) collective-permute-start(bf16[476,256]{1,0:T(8,128)(2,1)S(1)} %collective-permute-done.19), channel_id=1, source_target_pairs={{8,0},{16,8},{24,16},{28,24},{20,28},{12,20},{4,12},{0,4},{9,1},{1... | collective-permute-start | bytes 731144 | tf_op jit(solution)/shard_map/ppermute | solution.py:99
  120.4 10.6 %collective-permute-start.22 = (bf16[476,256]{1,0:T(8,128)(2,1)S(1)}, bf16[476,256]{1,0:T(8,128)(2,1)S(1)}, u32[]{:S(2)}, u32[]{:S(2)}) collective-permute-start(bf16[476,256]{1,0:T(8,128)(2,1)S(1)} %collective-permute-done.20), channel_id=1, source_target_pairs={{0,8},{8,16},{16,24},{24,28},{28,20},{20,12},{12,4},{4,0},{1,9},{9... | collective-permute-start | bytes 731144 | tf_op jit(solution)/shard_map/ppermute | solution.py:96
  139.0 11.0 %collective-permute-start.39 = (bf16[128,128]{1,0:T(8,128)(2,1)S(1)}, bf16[128,128]{1,0:T(8,128)(2,1)S(1)}, u32[]{:S(2)}, u32[]{:S(2)}) collective-permute-start(bf16[128,128]{1,0:T(8,128)(2,1)S(1)} %copy-done.84), channel_id=1, source_target_pairs={{8,0},{16,8},{24,16},{28,24},{20,28},{12,20},{4,12},{0,4},{9,1},{1... | collective-permute-start | bytes 98312 | tf_op jit(solution)/shard_map/ppermute | solution.py:99
  141.9 12.8 %collective-permute-start.25 = (bf16[8,476,256]{2,0,1:T(8,128)(2,1)}, bf16[8,476,256]{2,0,1:T(8,128)(2,1)}, u32[]{:S(2)}, u32[]{:S(2)}) collective-permute-start(bf16[8,476,256]{2,0,1:T(8,128)(2,1)} %copy.96), channel_id=1, source_target_pairs={{0,1},{1,0},{2,3},{3,2},{4,5},{5,4},{6,7},{7,6},{8,9},{9,8},{10,11... | collective-permute-start | bytes 5849096 | tf_op jit(solution)/shard_map/ppermute | solution.py:32
  148.6 150.0 %collective-permute-start.49 = (bf16[512,512]{1,0:T(8,128)(2,1)}, bf16[512,512]{1,0:T(8,128)(2,1)}, u32[]{:S(2)}, u32[]{:S(2)}) collective-permute-start(bf16[512,512]{1,0:T(8,128)(2,1)} %param.73), channel_id=1, source_target_pairs={{0,2},{1,3},{2,0},{3,1},{4,6},{5,7},{6,4},{7,5},{8,10},{9,11},{10,... | collective-permute-start | bytes 1572872 | tf_op jit(solution)/shard_map/ppermute | solution.py:32
  154.0 147.4 %collective-permute-start.52 = (bf16[512,512]{1,0:T(8,128)(2,1)}, bf16[512,512]{1,0:T(8,128)(2,1)}, u32[]{:S(2)}, u32[]{:S(2)}) collective-permute-start(bf16[512,512]{1,0:T(8,128)(2,1)} %param.74), channel_id=1, source_target_pairs={{0,2},{1,3},{2,0},{3,1},{4,6},{5,7},{6,4},{7,5},{8,10},{9,11},{10,... | collective-permute-start | bytes 1572872 | tf_op jit(solution)/shard_map/ppermute | solution.py:32
  154.7 96.5 %collective-permute-start.41 = (bf16[128,128]{1,0:T(8,128)(2,1)S(1)}, bf16[128,128]{1,0:T(8,128)(2,1)S(1)}, u32[]{:S(2)}, u32[]{:S(2)}) collective-permute-start(bf16[128,128]{1,0:T(8,128)(2,1)S(1)} %collective-permute-done.39), channel_id=1, source_target_pairs={{8,0},{16,8},{24,16},{28,24},{20,28},{12,20},{4,12},{0,4},{9,1},{1... | collective-permute-start | bytes 98312 | tf_op jit(solution)/shard_map/ppermute | solution.py:99
  246.7 56.0 %all-to-all-start = ((bf16[8,476,128]{2,1,0:T(8,128)(2,1)}), bf16[8,476,128]{2,1,0:T(8,128)(2,1)S(1)}, u32[]{:S(2)}, u32[]{:S(2)}) async-start(bf16[8,476,128]{2,1,0:T(8,128)(2,1)} %copy.105), calls=%async_computation | async-start | bytes 1966080 | tf_op jit(solution)/shard_map/all_to_all | solution.py:107
  251.2 473.1 %reduce-scatter.15.cloned.1.call-start = ((), (), s32[]{:S(2)}) async-start(), calls=%async_computation.14 | async-start | bytes 294912 | tf_op jit(solution)/shard_map/reduce_scatter | solution.py:112
  251.2 15.7 %collective-permute-start.42 = (bf16[128,128]{1,0:T(8,128)(2,1)S(1)}, bf16[128,128]{1,0:T(8,128)(2,1)S(1)}, u32[]{:S(2)}, u32[]{:S(2)}) collective-permute-start(bf16[128,128]{1,0:T(8,128)(2,1)S(1)} %collective-permute-done.40), channel_id=1, source_target_pairs={{0,8},{8,16},{16,24},{24,28},{28,20},{20,12},{12,4},{4,0},{1,9},{9... | collective-permute-start | bytes 98312 | tf_op jit(solution)/shard_map/ppermute | solution.py:96
  282.5 12.2 %collective-permute-start.46 = (bf16[1024,128]{1,0:T(8,128)(2,1)S(1)}, bf16[1024,128]{1,0:T(8,128)(2,1)S(1)}, u32[]{:S(2)}, u32[]{:S(2)}) collective-permute-start(bf16[1024,128]{1,0:T(8,128)(2,1)S(1)} %bitcast.286), channel_id=1, source_target_pairs={{0,2},{1,3},{2,0},{3,1},{4,6},{5,7},{6,4},{7,5},{8,10},{9,11},{10,... | collective-permute-start | bytes 786440 | tf_op jit(solution)/shard_map/ppermute | solution.py:32
  283.6 14.8 %collective-permute-start.59 = (bf16[816,128]{1,0:T(8,128)(2,1)S(1)}, bf16[816,128]{1,0:T(8,128)(2,1)S(1)}, u32[]{:S(2)}, u32[]{:S(2)}) collective-permute-start(bf16[816,128]{1,0:T(8,128)(2,1)S(1)} %copy-done.81), channel_id=1, source_target_pairs={{0,3},{1,2},{2,1},{3,0},{4,7},{5,6},{6,5},{7,4},{8,11},{9,10},{10,... | collective-permute-start | bytes 626696 | tf_op jit(solution)/shard_map/ppermute | solution.py:32
  289.1 12.0 %collective-permute-start.45 = (bf16[1024,128]{1,0:T(8,128)(2,1)S(1)}, bf16[1024,128]{1,0:T(8,128)(2,1)S(1)}, u32[]{:S(2)}, u32[]{:S(2)}) collective-permute-start(bf16[1024,128]{1,0:T(8,128)(2,1)S(1)} %bitcast.287), channel_id=1, source_target_pairs={{0,1},{1,0},{2,3},{3,2},{4,5},{5,4},{6,7},{7,6},{8,9},{9,8},{10,11... | collective-permute-start | bytes 786440 | tf_op jit(solution)/shard_map/ppermute | solution.py:32
  301.1 10.0 %collective-permute-start.51 = (bf16[512,512]{1,0:T(8,128)(2,1)S(1)}, bf16[512,512]{1,0:T(8,128)(2,1)S(1)}, u32[]{:S(2)}, u32[]{:S(2)}) collective-permute-start(bf16[512,512]{1,0:T(8,128)(2,1)S(1)} %copy-done.67), channel_id=1, source_target_pairs={{0,1},{1,0},{2,3},{3,2},{4,5},{5,4},{6,7},{7,6},{8,9},{9,8},{10,11... | collective-permute-start | bytes 1572872 | tf_op jit(solution)/shard_map/ppermute | solution.py:32
  328.0 10.3 %collective-permute-start.37 = (bf16[816,128]{1,0:T(8,128)(2,1)}, bf16[816,128]{1,0:T(8,128)(2,1)}, u32[]{:S(2)}, u32[]{:S(2)}) collective-permute-start(bf16[816,128]{1,0:T(8,128)(2,1)} %get-tuple-element.420), channel_id=1, source_target_pairs={{0,3},{1,2},{2,1},{3,0},{4,7},{5,6},{6,5},{7,4},{8,11},{9,10},{10,... | collective-permute-start | bytes 626696 | tf_op jit(solution)/shard_map/ppermute | solution.py:32
  332.7 11.2 %collective-permute-start.33 = (bf16[816,128]{1,0:T(8,128)(2,1)S(1)}, bf16[816,128]{1,0:T(8,128)(2,1)S(1)}, u32[]{:S(2)}, u32[]{:S(2)}) collective-permute-start(bf16[816,128]{1,0:T(8,128)(2,1)S(1)} %get-tuple-element.424), channel_id=1, source_target_pairs={{0,2},{1,3},{2,0},{3,1},{4,6},{5,7},{6,4},{7,5},{8,10},{9,11},{10,... | collective-permute-start | bytes 626696 | tf_op jit(solution)/shard_map/ppermute | solution.py:32
  334.1 12.3 %collective-permute-start.34 = (bf16[816,128]{1,0:T(8,128)(2,1)S(1)}, bf16[816,128]{1,0:T(8,128)(2,1)S(1)}, u32[]{:S(2)}, u32[]{:S(2)}) collective-permute-start(bf16[816,128]{1,0:T(8,128)(2,1)S(1)} %get-tuple-element.423), channel_id=1, source_target_pairs={{0,3},{1,2},{2,1},{3,0},{4,7},{5,6},{6,5},{7,4},{8,11},{9,10},{10,... | collective-permute-start | bytes 626696 | tf_op jit(solution)/shard_map/ppermute | solution.py:32
  400.7 10.0 %collective-permute-start.62 = (bf16[816,128]{1,0:T(8,128)(2,1)S(1)}, bf16[816,128]{1,0:T(8,128)(2,1)S(1)}, u32[]{:S(2)}, u32[]{:S(2)}) collective-permute-start(bf16[816,128]{1,0:T(8,128)(2,1)S(1)} %get-tuple-element.411), channel_id=1, source_target_pairs={{0,3},{1,2},{2,1},{3,0},{4,7},{5,6},{6,5},{7,4},{8,11},{9,10},{10,... | collective-permute-start | bytes 626696 | tf_op jit(solution)/shard_map/ppermute | solution.py:32
  402.5 17.9 %collective-permute-start.63 = (bf16[816,128]{1,0:T(8,128)(2,1)}, bf16[816,128]{1,0:T(8,128)(2,1)}, u32[]{:S(2)}, u32[]{:S(2)}) collective-permute-start(bf16[816,128]{1,0:T(8,128)(2,1)} %get-tuple-element.412), channel_id=1, source_target_pairs={{0,1},{1,0},{2,3},{3,2},{4,5},{5,4},{6,7},{7,6},{8,9},{9,8},{10,11... | collective-permute-start | bytes 626696 | tf_op jit(solution)/shard_map/ppermute | solution.py:32
  403.2 17.2 %collective-permute-start.64 = (bf16[816,128]{1,0:T(8,128)(2,1)}, bf16[816,128]{1,0:T(8,128)(2,1)}, u32[]{:S(2)}, u32[]{:S(2)}) collective-permute-start(bf16[816,128]{1,0:T(8,128)(2,1)} %get-tuple-element.329), channel_id=1, source_target_pairs={{0,2},{1,3},{2,0},{3,1},{4,6},{5,7},{6,4},{7,5},{8,10},{9,11},{10,... | collective-permute-start | bytes 626696 | tf_op jit(solution)/shard_map/ppermute | solution.py:32
  407.8 13.1 %collective-permute-start.65 = (bf16[816,128]{1,0:T(8,128)(2,1)}, bf16[816,128]{1,0:T(8,128)(2,1)}, u32[]{:S(2)}, u32[]{:S(2)}) collective-permute-start(bf16[816,128]{1,0:T(8,128)(2,1)} %get-tuple-element.413), channel_id=1, source_target_pairs={{0,3},{1,2},{2,1},{3,0},{4,7},{5,6},{6,5},{7,4},{8,11},{9,10},{10,... | collective-permute-start | bytes 626696 | tf_op jit(solution)/shard_map/ppermute | solution.py:32
  407.8 25.2 %collective-permute-start.86 = (bf16[512,512]{1,0:T(8,128)(2,1)}, bf16[512,512]{1,0:T(8,128)(2,1)}, u32[]{:S(2)}, u32[]{:S(2)}) collective-permute-start(bf16[512,512]{1,0:T(8,128)(2,1)} %get-tuple-element.342), channel_id=1, source_target_pairs={{0,1},{1,0},{2,3},{3,2},{4,5},{5,4},{6,7},{7,6},{8,9},{9,8},{10,11... | collective-permute-start | bytes 1572872 | tf_op jit(solution)/shard_map/ppermute | solution.py:32
  410.7 54.8 %collective-permute-start.85 = (bf16[512,512]{1,0:T(8,128)(2,1)}, bf16[512,512]{1,0:T(8,128)(2,1)}, u32[]{:S(2)}, u32[]{:S(2)}) collective-permute-start(bf16[512,512]{1,0:T(8,128)(2,1)} %get-tuple-element.341), channel_id=1, source_target_pairs={{0,1},{1,0},{2,3},{3,2},{4,5},{5,4},{6,7},{7,6},{8,9},{9,8},{10,11... | collective-permute-start | bytes 1572872 | tf_op jit(solution)/shard_map/ppermute | solution.py:32
  420.4 18.3 %collective-permute-start.89 = (bf16[512,512]{1,0:T(8,128)(2,1)}, bf16[512,512]{1,0:T(8,128)(2,1)}, u32[]{:S(2)}, u32[]{:S(2)}) collective-permute-start(bf16[512,512]{1,0:T(8,128)(2,1)} %get-tuple-element.344), channel_id=1, source_target_pairs={{0,1},{1,0},{2,3},{3,2},{4,5},{5,4},{6,7},{7,6},{8,9},{9,8},{10,11... | collective-permute-start | bytes 1572872 | tf_op jit(solution)/shard_map/ppermute | solution.py:32
  420.4 10.8 %collective-permute-start.83 = (bf16[1024,128]{1,0:T(8,128)(2,1)}, bf16[1024,128]{1,0:T(8,128)(2,1)}, u32[]{:S(2)}, u32[]{:S(2)}) collective-permute-start(bf16[1024,128]{1,0:T(8,128)(2,1)} %get-tuple-element.354), channel_id=1, source_target_pairs={{0,1},{1,0},{2,3},{3,2},{4,5},{5,4},{6,7},{7,6},{8,9},{9,8},{10,11... | collective-permute-start | bytes 786440 | tf_op jit(solution)/shard_map/ppermute | solution.py:32
  420.9 21.3 %collective-permute-start.82 = (bf16[1024,128]{1,0:T(8,128)(2,1)}, bf16[1024,128]{1,0:T(8,128)(2,1)}, u32[]{:S(2)}, u32[]{:S(2)}) collective-permute-start(bf16[1024,128]{1,0:T(8,128)(2,1)} %get-tuple-element.353), channel_id=1, source_target_pairs={{0,1},{1,0},{2,3},{3,2},{4,5},{5,4},{6,7},{7,6},{8,9},{9,8},{10,11... | collective-permute-start | bytes 786440 | tf_op jit(solution)/shard_map/ppermute | solution.py:32
  436.9 28.6 %collective-permute-start.87 = (bf16[512,512]{1,0:T(8,128)(2,1)}, bf16[512,512]{1,0:T(8,128)(2,1)}, u32[]{:S(2)}, u32[]{:S(2)}) collective-permute-start(bf16[512,512]{1,0:T(8,128)(2,1)} %add_convert_fusion.11), channel_id=1, source_target_pairs={{0,2},{1,3},{2,0},{3,1},{4,6},{5,7},{6,4},{7,5},{8,10},{9,11},{10,... | collective-permute-start | bytes 1572872 | tf_op jit(solution)/shard_map/ppermute | solution.py:32
  438.7 25.5 %collective-permute-start.67 = (f32[476,256]{1,0:T(8,128)}, f32[476,256]{1,0:T(8,128)}, u32[]{:S(2)}, u32[]{:S(2)}) collective-permute-start(f32[476,256]{1,0:T(8,128)} %maximum_add_fusion), channel_id=1, source_target_pairs={{0,2},{1,3},{2,0},{3,1},{4,6},{5,7},{6,4},{7,5},{8,10},{9,11},{10,... | collective-permute-start | bytes 1462280 | tf_op jit(solution)/shard_map/ppermute | solution.py:32
  442.2 26.6 %collective-permute-start.88 = (bf16[512,512]{1,0:T(8,128)(2,1)}, bf16[512,512]{1,0:T(8,128)(2,1)}, u32[]{:S(2)}, u32[]{:S(2)}) collective-permute-start(bf16[512,512]{1,0:T(8,128)(2,1)} %get-tuple-element.343), channel_id=1, source_target_pairs={{0,1},{1,0},{2,3},{3,2},{4,5},{5,4},{6,7},{7,6},{8,9},{9,8},{10,11... | collective-permute-start | bytes 1572872 | tf_op jit(solution)/shard_map/ppermute | solution.py:32
  442.3 32.1 %collective-permute-start.90 = (bf16[512,512]{1,0:T(8,128)(2,1)}, bf16[512,512]{1,0:T(8,128)(2,1)}, u32[]{:S(2)}, u32[]{:S(2)}) collective-permute-start(bf16[512,512]{1,0:T(8,128)(2,1)} %add_convert_fusion.9), channel_id=1, source_target_pairs={{0,2},{1,3},{2,0},{3,1},{4,6},{5,7},{6,4},{7,5},{8,10},{9,11},{10,... | collective-permute-start | bytes 1572872 | tf_op jit(solution)/shard_map/ppermute | solution.py:32
  445.5 376.5 %reduce-scatter.17.cloned.1.call-start = ((), (), s32[]{:S(2)}) async-start(), calls=%async_computation.15 | async-start | bytes 1179648 | tf_op jit(solution)/shard_map/reduce_scatter | solution.py:112
  465.4 11.9 %collective-permute-start.68 = (f32[476,256]{1,0:T(8,128)S(1)}, f32[476,256]{1,0:T(8,128)S(1)}, u32[]{:S(2)}, u32[]{:S(2)}) collective-permute-start(f32[476,256]{1,0:T(8,128)S(1)} %add.1169), channel_id=1, source_target_pairs={{0,1},{1,0},{2,3},{3,2},{4,5},{5,4},{6,7},{7,6},{8,9},{9,8},{10,11... | collective-permute-start | bytes 1462280 | tf_op jit(solution)/shard_map/ppermute | solution.py:32
  477.3 397.0 %reduce-scatter.9.cloned.1.call-start = ((), (), s32[]{:S(2)}) async-start(), calls=%async_computation.11 | async-start | bytes 1769472 | tf_op jit(solution)/shard_map/reduce_scatter | solution.py:112
  486.9 26.0 %collective-permute-start.72 = (bf16[476,128]{1,0:T(8,128)(2,1)S(1)}, bf16[476,128]{1,0:T(8,128)(2,1)S(1)}, u32[]{:S(2)}, u32[]{:S(2)}) collective-permute-start(bf16[476,128]{1,0:T(8,128)(2,1)S(1)} %collective-permute-done.70), channel_id=1, source_target_pairs={{8,0},{16,8},{24,16},{28,24},{20,28},{12,20},{4,12},{0,4},{9,1},{1... | collective-permute-start | bytes 365576 | tf_op jit(solution)/shard_map/ppermute | solution.py:99
  491.0 23.3 %collective-permute-start.73 = (bf16[476,128]{1,0:T(8,128)(2,1)S(1)}, bf16[476,128]{1,0:T(8,128)(2,1)S(1)}, u32[]{:S(2)}, u32[]{:S(2)}) collective-permute-start(bf16[476,128]{1,0:T(8,128)(2,1)S(1)} %collective-permute-done.71), channel_id=1, source_target_pairs={{0,8},{8,16},{16,24},{24,28},{28,20},{20,12},{12,4},{4,0},{1,9},{9... | collective-permute-start | bytes 365576 | tf_op jit(solution)/shard_map/ppermute | solution.py:96
  512.9 38.2 %collective-permute-start.74 = (bf16[476,128]{1,0:T(8,128)(2,1)S(1)}, bf16[476,128]{1,0:T(8,128)(2,1)S(1)}, u32[]{:S(2)}, u32[]{:S(2)}) collective-permute-start(bf16[476,128]{1,0:T(8,128)(2,1)S(1)} %collective-permute-done.72), channel_id=1, source_target_pairs={{8,0},{16,8},{24,16},{28,24},{20,28},{12,20},{4,12},{0,4},{9,1},{1... | collective-permute-start | bytes 365576 | tf_op jit(solution)/shard_map/ppermute | solution.py:99
  514.2 49.9 %collective-permute-start.75 = (bf16[476,128]{1,0:T(8,128)(2,1)S(1)}, bf16[476,128]{1,0:T(8,128)(2,1)S(1)}, u32[]{:S(2)}, u32[]{:S(2)}) collective-permute-start(bf16[476,128]{1,0:T(8,128)(2,1)S(1)} %collective-permute-done.73), channel_id=1, source_target_pairs={{0,8},{8,16},{16,24},{24,28},{28,20},{20,12},{12,4},{4,0},{1,9},{9... | collective-permute-start | bytes 365576 | tf_op jit(solution)/shard_map/ppermute | solution.py:96
  517.7 372.3 %reduce-scatter.13.cloned.1.call-start = ((), (), s32[]{:S(2)}) async-start(), calls=%async_computation.13 | async-start | bytes 2359296 | tf_op jit(solution)/shard_map/reduce_scatter | solution.py:112
  704.4 14.4 %collective-permute-start.77 = (bf16[8,476,128]{2,0,1:T(8,128)(2,1)}, bf16[8,476,128]{2,0,1:T(8,128)(2,1)S(1)}, u32[]{:S(2)}, u32[]{:S(2)}) collective-permute-start(bf16[8,476,128]{2,0,1:T(8,128)(2,1)} %select_convert_fusion), channel_id=1, source_target_pairs={{0,1},{1,0},{2,3},{3,2},{4,5},{5,4},{6,7},{7,6},{8,9},{9,8},{10,11... | collective-permute-start | bytes 2924552 | tf_op jit(solution)/shard_map/ppermute | solution.py:32
  718.1 54.7 %collective-permute-start.76 = (bf16[8,476,128]{2,0,1:T(8,128)(2,1)}, bf16[8,476,128]{2,0,1:T(8,128)(2,1)}, u32[]{:S(2)}, u32[]{:S(2)}) collective-permute-start(bf16[8,476,128]{2,0,1:T(8,128)(2,1)} %get-tuple-element.319), channel_id=1, source_target_pairs={{0,1},{1,0},{2,3},{3,2},{4,5},{5,4},{6,7},{7,6},{8,9},{9,8},{10,11... | collective-permute-start | bytes 2924552 | tf_op jit(solution)/shard_map/ppermute | solution.py:32
  721.6 51.1 %collective-permute-start.78 = (bf16[8,476,128]{2,0,1:T(8,128)(2,1)}, bf16[8,476,128]{2,0,1:T(8,128)(2,1)S(1)}, u32[]{:S(2)}, u32[]{:S(2)}) collective-permute-start(bf16[8,476,128]{2,0,1:T(8,128)(2,1)} %add_convert_fusion.2), channel_id=1, source_target_pairs={{0,2},{1,3},{2,0},{3,1},{4,6},{5,7},{6,4},{7,5},{8,10},{9,11},{10,... | collective-permute-start | bytes 2924552 | tf_op jit(solution)/shard_map/ppermute | solution.py:32
  776.2 28.1 %all-to-all-start.1 = ((bf16[8,476,128]{2,1,0:T(8,128)(2,1)}), bf16[8,476,128]{2,1,0:T(8,128)(2,1)}, u32[]{:S(2)}, u32[]{:S(2)}) async-start(bf16[8,476,128]{2,1,0:T(8,128)(2,1)} %copy.120), calls=%async_computation.1 | async-start | bytes 1966080 | tf_op jit(solution)/shard_map/all_to_all | solution.py:107
  780.5 135.6 %reduce-scatter.7.cloned.1.call-start = ((), (), s32[]{:S(2)}) async-start(), calls=%async_computation.10 | async-start | bytes 1769472 | tf_op jit(solution)/shard_map/reduce_scatter | solution.py:112
  810.2 135.6 %reduce-scatter.11.cloned.1.call-start = ((), (), s32[]{:S(2)}) async-start(), calls=%async_computation.12 | async-start | bytes 2359296 | tf_op jit(solution)/shard_map/reduce_scatter | solution.py:112
  827.3 48.7 %collective-permute-start.93 = (bf16[128,512]{1,0:T(8,128)(2,1)}, bf16[128,512]{1,0:T(8,128)(2,1)S(1)}, u32[]{:S(2)}, u32[]{:S(2)}) collective-permute-start(bf16[128,512]{1,0:T(8,128)(2,1)} %collective-permute-done.91), channel_id=1, source_target_pairs={{0,8},{8,16},{16,24},{24,28},{28,20},{20,12},{12,4},{4,0},{1,9},{9... | collective-permute-start | bytes 393224 | tf_op jit(solution)/shard_map/ppermute | solution.py:96
  829.7 46.3 %collective-permute-start.94 = (bf16[128,512]{1,0:T(8,128)(2,1)}, bf16[128,512]{1,0:T(8,128)(2,1)S(1)}, u32[]{:S(2)}, u32[]{:S(2)}) collective-permute-start(bf16[128,512]{1,0:T(8,128)(2,1)} %collective-permute-done.92), channel_id=1, source_target_pairs={{8,0},{16,8},{24,16},{28,24},{20,28},{12,20},{4,12},{0,4},{9,1},{1... | collective-permute-start | bytes 393224 | tf_op jit(solution)/shard_map/ppermute | solution.py:99
  872.4 9.8 %collective-permute-start.80 = (bf16[3264,128]{1,0:T(8,128)(2,1)S(1)}, bf16[3264,128]{1,0:T(8,128)(2,1)S(1)}, u32[]{:S(2)}, u32[]{:S(2)}) collective-permute-start(bf16[3264,128]{1,0:T(8,128)(2,1)S(1)} %get-tuple-element.340), channel_id=1, source_target_pairs={{0,1},{1,0},{2,3},{3,2},{4,5},{5,4},{6,7},{7,6},{8,9},{9,8},{10,11... | collective-permute-start | bytes 2506760 | tf_op jit(solution)/shard_map/ppermute | solution.py:32
  876.0 12.3 %collective-permute-start.96 = (bf16[128,512]{1,0:T(8,128)(2,1)S(1)}, bf16[128,512]{1,0:T(8,128)(2,1)S(1)}, u32[]{:S(2)}, u32[]{:S(2)}) collective-permute-start(bf16[128,512]{1,0:T(8,128)(2,1)S(1)} %collective-permute-done.94), channel_id=1, source_target_pairs={{8,0},{16,8},{24,16},{28,24},{20,28},{12,20},{4,12},{0,4},{9,1},{1... | collective-permute-start | bytes 393224 | tf_op jit(solution)/shard_map/ppermute | solution.py:99
  886.4 21.4 %collective-permute-start.81 = (bf16[3264,128]{1,0:T(8,128)(2,1)}, bf16[3264,128]{1,0:T(8,128)(2,1)}, u32[]{:S(2)}, u32[]{:S(2)}) collective-permute-start(bf16[3264,128]{1,0:T(8,128)(2,1)} %add_convert_fusion.3), channel_id=1, source_target_pairs={{0,2},{1,3},{2,0},{3,1},{4,6},{5,7},{6,4},{7,5},{8,10},{9,11},{10,... | collective-permute-start | bytes 2506760 | tf_op jit(solution)/shard_map/ppermute | solution.py:32
  (150 other events, 1372.1 us)
Sparse Core Ops, SparseCore 0:
  14.0 51.2 all-gather.2
  109.0 53.3 all-gather.4
  445.6 60.8 reduce-scatter.14
  510.4 62.5 reduce-scatter.16
  577.3 64.7 reduce-scatter.8
  711.0 68.7 reduce-scatter.12
  810.3 65.0 reduce-scatter.6
  879.4 66.3 reduce-scatter.10
